TPU v7x, 32 devices: a whole 2x2x4 slice. The times are simulated.
32 devices in a mesh: expert: 8 (over z, x), dp: 4 (over y, core).
Axes of the slice: x: 2, y: 2, z: 4, core: 2. Of those that a mesh axis runs over, the one named last changes fastest.
Arguments:
- tokens: bfloat16 [1024, 7168], P('expert'), may hold values from -6 to 6
- routes: int32 [1024, 2], P('expert'), may hold values from 0 to 7, all different within a row; in each aligned block of 128 rows (0 to 127, 128 to 255, ...) at most 96 rows name the same one
- route_gates: bfloat16 [1024, 2], P('expert'), may hold values from 0.049804688 to 1
- cotangent: bfloat16 [1024, 7168], P('expert'), may hold values from -6 to 6
- weight_gate: bfloat16 [8, 7168, 1024], P('expert', None, 'dp'), may hold values from -0.0625 to 0.0625
- weight_up: bfloat16 [8, 7168, 1024], P('expert', None, 'dp'), may hold values from -0.0625 to 0.0625
- weight_down: bfloat16 [8, 1024, 7168], P('expert', 'dp'), may hold values from -0.1875 to 0.1875
Outputs:
- grad_tokens: bfloat16 [1024, 7168], P('expert', 'dp')
- grad_gate: bfloat16 [8, 7168, 1024], P('expert', None, 'dp')
- grad_up: bfloat16 [8, 7168, 1024], P('expert', None, 'dp')
- grad_down: bfloat16 [8, 1024, 7168], P('expert', 'dp')
Inputs may be any that keep to these rules, and one draw needn't show every extreme that they name: `routes`: within each aligned block of 128 rows (the tokens of one index of the expert axis) every row names 2 different experts and no expert is named by more than 96 rows; in every draw some block names some expert exactly 96 times.
All inputs are finite; a program needn't handle non-finite values.
Results may differ from a plain program's by a relative error of at most 0.011.
Values may be sent and summed in bfloat16 or wider, within the bound.
A program may use at most 192 MiB of HBM per device.

v0:
```python
import jax
import jax.numpy as jnp
from jax import lax
from jax.sharding import PartitionSpec as P


def slot_layout(routes, experts, capacity):
    flat_routes = routes.reshape(-1)
    onehot = (flat_routes[:, None] == jnp.arange(experts, dtype=jnp.int32)[None, :]).astype(
        jnp.int32
    )
    before = jnp.cumsum(onehot, axis=0) - onehot
    position = jnp.sum(before * onehot, axis=1)
    slot_index = flat_routes * capacity + position
    total_slots = flat_routes.shape[0]
    owners = (
        jnp.full((experts * capacity,), total_slots, dtype=jnp.int32)
        .at[slot_index]
        .set(jnp.arange(total_slots, dtype=jnp.int32))
    )
    return (slot_index, owners)


def pad_rows(source_array, owners, top_count):
    extended = jnp.concatenate(
        [source_array, jnp.zeros((1,) + source_array.shape[1:], source_array.dtype)], 0
    )
    return extended[owners // top_count]


def per_device(tokens, routes, route_gates, cotangent, weight_gate, weight_up, weight_down):
    members = lax.axis_size("expert")
    groups = lax.axis_size("dp")
    local_experts = weight_gate.shape[0]
    experts = members * local_experts
    token_rows = routes.shape[0]
    top_count = routes.shape[1]
    width = tokens.shape[1]
    quarter = width // groups
    capacity = 3 * token_rows * top_count // experts
    slot_index, owners = slot_layout(routes, experts, capacity)
    gate_flat = jnp.concatenate([route_gates.reshape(-1), jnp.zeros((1,), route_gates.dtype)], 0)
    gate_send = gate_flat[owners].reshape(experts, capacity)
    token_send = pad_rows(tokens, owners, top_count).reshape(experts, capacity, width)
    back_send = pad_rows(cotangent, owners, top_count).reshape(experts, capacity, width)
    token_arrived, back_arrived, gate_arrived = (
        lax.all_to_all(token_send, "expert", split_axis=0, concat_axis=1, tiled=True),
        lax.all_to_all(back_send, "expert", split_axis=0, concat_axis=1, tiled=True),
        lax.all_to_all(gate_send, "expert", split_axis=0, concat_axis=1, tiled=True),
    )
    scale = gate_arrived.astype(jnp.float32)[:, :, None]
    pre_gate = jnp.einsum(
        "erd,edf->erf", token_arrived, weight_gate, preferred_element_type=jnp.float32
    )
    pre_up = jnp.einsum(
        "erd,edf->erf", token_arrived, weight_up, preferred_element_type=jnp.float32
    )
    sigma = jax.nn.sigmoid(pre_gate)
    activated = pre_gate * sigma
    scaled_hidden = (scale * activated * pre_up).astype(jnp.bfloat16)
    back_hidden = scale * jnp.einsum(
        "erd,efd->erf", back_arrived, weight_down, preferred_element_type=jnp.float32
    )
    back_up = (back_hidden * activated).astype(jnp.bfloat16)
    back_gate = (back_hidden * pre_up * sigma * (1.0 + pre_gate * (1.0 - sigma))).astype(
        jnp.bfloat16
    )
    grad_gate = jnp.einsum(
        "erd,erf->edf", token_arrived, back_gate, preferred_element_type=jnp.float32
    ).astype(jnp.bfloat16)
    grad_up = jnp.einsum(
        "erd,erf->edf", token_arrived, back_up, preferred_element_type=jnp.float32
    ).astype(jnp.bfloat16)
    grad_down = jnp.einsum(
        "erf,erd->efd", scaled_hidden, back_arrived, preferred_element_type=jnp.float32
    ).astype(jnp.bfloat16)
    up_term = jnp.einsum("edf,erf->der", weight_up, back_up, preferred_element_type=jnp.float32)
    gate_term = jnp.einsum(
        "edf,erf->der", weight_gate, back_gate, preferred_element_type=jnp.float32
    )
    slot_back = lax.psum_scatter(
        (up_term + gate_term).astype(jnp.bfloat16), "dp", scatter_dimension=0, tiled=True
    )
    returned = lax.all_to_all(slot_back, "expert", split_axis=2, concat_axis=1, tiled=True)
    flat_back = returned.reshape(quarter, experts * capacity)
    picked = (
        jnp.take(flat_back, slot_index, axis=1)
        .astype(jnp.float32)
        .reshape(quarter, token_rows, top_count)
    )
    grad_tokens = jnp.sum(picked, axis=2).T.astype(jnp.bfloat16)
    return (grad_tokens, grad_gate, grad_up, grad_down)


def solution(mesh):
    placed = (
        P("expert", None),
        P("expert", None),
        P("expert", None),
        P("expert", None),
        P("expert", None, "dp"),
        P("expert", None, "dp"),
        P("expert", "dp", None),
    )
    return jax.shard_map(
        per_device,
        mesh=mesh,
        in_specs=placed,
        out_specs=(
            P("expert", "dp"),
            P("expert", None, "dp"),
            P("expert", None, "dp"),
            P("expert", "dp", None),
        ),
        check_vma=False,
    )
```

profile of v0, /device:TPU:20, one launch (start us, length us, event | category | flops | bytes accessed | tf_op | source)
XLA Modules:
  0.0 764.7 jit_solution(8576594936999472891)
XLA Ops:
  7.2 0.7 broadcast_multiply_fusion
  7.8 0.8 copy.30
  8.6 0.1 eq.26
  8.8 0.1 reshape.180
  8.9 0.8 copy.34
  9.7 0.1 reshape.182
  9.9 0.1 copy.35
  10.0 0.1 mul.69
  10.1 0.6 reduce-window.6
  10.7 0.2 slice_reduce_fusion
  11.0 0.1 fusion.21
  11.1 1.4 scatter_custom_fusion
  12.5 5.0 gather_fusion
  17.5 0.7 all_to_all.16
  18.2 6.1 all-to-all-start
  24.4 1.7 concatenate.11
  26.1 9.4 %gather_fusion.2 = bf16[768,7168]{1,0:T(8,128)(2,1)} fusion(bf16[129,7168]{1,0:T(8,128)(2,1)S(1)} %concatenate.11, s32[1024]{0:T(1024)S(1)} %get-tuple-element.9), kind=kCustom, calls=%fused_computation.2 | custom fusion | bytes 22023168 | tf_op jit(solution)/shard_map/gather | solution.py:28
  35.5 0.0 all-to-all-done
  35.5 6.0 all-to-all-start.2
  41.5 1.7 concatenate.10
  43.1 9.5 %gather_fusion.1 = bf16[768,7168]{1,0:T(8,128)(2,1)} fusion(bf16[129,7168]{1,0:T(8,128)(2,1)S(1)} %concatenate.10, s32[1024]{0:T(1024)S(1)} %get-tuple-element.9), kind=kCustom, calls=%fused_computation.1 | custom fusion | bytes 22023168 | tf_op jit(solution)/shard_map/gather | solution.py:28
  52.6 224.3 %all-to-all-done.2 = bf16[8,96,7168]{2,1,0:T(8,128)(2,1)} async-done(((bf16[8,96,7168]{2,1,0:T(8,128)(2,1)}), bf16[8,96,7168]{2,1,0:T(8,128)(2,1)}, u32[]{:S(2)}, u32[]{:S(2)}) %all-to-all-start.2) | async-done | bytes 11010080 | tf_op jit(solution)/shard_map/all_to_all | solution.py:47
  276.9 8.5 %all-to-all-start.1 = ((bf16[8,96,7168]{2,1,0:T(8,128)(2,1)}), bf16[8,96,7168]{2,1,0:T(8,128)(2,1)}, u32[]{:S(2)}, u32[]{:S(2)}) async-start(bf16[8,96,7168]{2,1,0:T(8,128)(2,1)} %bitcast.64), calls=%async_computation.1 | async-start | bytes 22020096 | tf_op jit(solution)/shard_map/all_to_all | solution.py:48
  285.4 0.5 reduce-scatter.2.cloned.1.call-start
  285.9 0.1 reshape.191
  286.0 6.9 fusion.4
  292.9 227.2 %all-to-all-done.1 = bf16[8,96,7168]{2,1,0:T(8,128)(2,1)} async-done(((bf16[8,96,7168]{2,1,0:T(8,128)(2,1)}), bf16[8,96,7168]{2,1,0:T(8,128)(2,1)}, u32[]{:S(2)}, u32[]{:S(2)}) %all-to-all-start.1) | async-done | bytes 11010080 | tf_op jit(solution)/shard_map/all_to_all | solution.py:48
  520.0 0.0 copy-start.1
  520.0 7.1 fusion.13
  527.1 0.0 copy-done.1
  527.1 0.0 copy-start
  527.1 8.3 %multiply_convert_fusion.1 = (bf16[768,256]{1,0:T(8,128)(2,1)S(1)}, bf16[768,256]{1,0:T(8,128)(2,1)S(1)}, f32[768,256]{1,0:T(8,128)}) fusion(f32[768,256]{1,0:T(8,128)S(1)} %fusion.13, f32[768,256]{1,0:T(8,128)S(1)} %fusion.4, bf16[768,7168]{1,0:T(8,128)(2,1)} %bitcast.8, bf16[1,7168,256]{2,1,0:T(8,128)(2,1)S(1)} %copy-done.1), kind=kOutput, calls=%fused_computation.27 | convolution fusion | flops 2821128192 | bytes 17825792 | tf_op jit(solution)/shard_map/erd,edf->erf/dot_general | solution.py:52
  535.5 0.0 copy-start.2
  535.5 0.0 copy-done
  535.5 9.1 %fusion.6 = f32[768,7168]{1,0:T(8,128)} fusion(bf16[768,256]{1,0:T(8,128)(2,1)S(1)} %get-tuple-element.5, bf16[1,7168,256]{2,1,0:T(8,128)(2,1)S(1)} %copy-done), kind=kOutput, calls=%fused_computation.15 | convolution fusion | flops 2818572288 | bytes 26083328 | tf_op jit(solution)/shard_map/edf,erf->der/dot_general | solution.py:77
  544.5 0.0 copy-done.4
  544.5 0.0 copy-done.2
  544.5 12.5 %fusion = bf16[7168,1,768]{0,2,1:T(8,128)(2,1)} fusion(f32[768,7168]{1,0:T(8,128)} %fusion.6, bf16[768,256]{1,0:T(8,128)(2,1)S(1)} %get-tuple-element.4, bf16[1,7168,256]{2,1,0:T(8,128)(2,1)S(1)} %copy-done.1), kind=kOutput, calls=%fused_computation.6 | convolution fusion | flops 2829582336 | bytes 37093376 | tf_op jit(solution)/shard_map/edf,erf->der/dot_general | solution.py:78
  557.0 0.0 reduce-scatter.2.cloned.1.call-update
  557.1 90.3 %reduce-scatter.2.cloned.1.call-done = bf16[1792,1,768]{0,2,1:T(8,128)(2,1)} async-done(((bf16[7168,1,768]{0,2,1:T(8,128)(2,1)}), bf16[1792,1,768]{0,2,1:T(8,128)(2,1)}) %reduce-scatter.2.cloned.1.call-update) | async-done | bytes 2752528 | tf_op jit(solution)/shard_map/reduce_scatter | solution.py:81
  647.4 8.4 %copy.44 = bf16[1792,1,768]{0,1,2:T(2,128)(2,1)} copy(bf16[1792,1,768]{0,2,1:T(8,128)(2,1)} %reduce-scatter.2.cloned.1.call-done) | data formatting | bytes 5505024 | tf_op jit(solution)/shard_map/reduce_scatter | solution.py:81
  655.8 0.5 broadcast.118
  656.3 17.0 %reduce.7 = bf16[768,1792]{1,0:T(8,128)(2,1)S(1)} reduce(bf16[768,1,1792]{2,1,0:T(2,128)(2,1)} %bitcast.67, bf16[]{:T(256)} %broadcast.118), dimensions={1}, to_apply=%bitcast.62.reduce_sub_computation | reduce | bytes 5505026
  673.3 0.0 copy-start.7
  673.3 3.5 reshape.245
  676.8 6.3 all-to-all-start.3
  683.1 0.8 reduce_sum.26
  683.8 0.9 copy.32
  684.7 0.0 copy-done.7
  684.7 0.5 compare_and_fusion
  685.3 1.4 copy.33
  686.6 0.0 copy-start.3
  686.6 9.5 %fusion.3 = bf16[1,256,7168]{2,1,0:T(8,128)(2,1)} fusion(bf16[768,7168]{1,0:T(8,128)(2,1)} %bitcast.5, f32[768,256]{1,0:T(8,128)S(1)} %fusion.4, f32[768]{0:T(1024)S(1)} %reshape.191, f32[768,256]{1,0:T(8,128)} %get-tuple-element.8), kind=kOutput, calls=%fused_computation.12 | convolution fusion | flops 2821783552 | bytes 16256000 | tf_op jit(solution)/shard_map/erf,erd->efd/dot_general | solution.py:74
  696.1 0.0 copy-done.3
  696.1 9.1 %fusion.1 = bf16[1,7168,256]{2,1,0:T(8,128)(2,1)} fusion(bf16[768,7168]{1,0:T(8,128)(2,1)} %bitcast.8, bf16[768,256]{1,0:T(8,128)(2,1)S(1)} %copy-done.3), kind=kOutput, calls=%fused_computation.10 | convolution fusion | flops 2820407296 | bytes 15073280 | tf_op jit(solution)/shard_map/erd,erf->edf/dot_general | solution.py:68
  705.3 0.0 copy-done.5
  705.3 9.1 %fusion.2 = bf16[1,7168,256]{2,1,0:T(8,128)(2,1)} fusion(bf16[768,7168]{1,0:T(8,128)(2,1)} %bitcast.8, bf16[768,256]{1,0:T(8,128)(2,1)S(1)} %copy-done.5), kind=kOutput, calls=%fused_computation.11 | convolution fusion | flops 2820407296 | bytes 15073280 | tf_op jit(solution)/shard_map/erd,erf->edf/dot_general | solution.py:71
  714.3 27.7 %all-to-all-done.3 = bf16[8,2,86016]{2,1,0:T(2,128)(2,1)S(1)} async-done(((bf16[8,2,86016]{2,1,0:T(2,128)(2,1)}), bf16[8,2,86016]{2,1,0:T(2,128)(2,1)S(1)}, u32[]{:S(2)}, u32[]{:S(2)}) %all-to-all-start.3) | async-done | bytes 2752544 | tf_op jit(solution)/shard_map/all_to_all | solution.py:84
  742.0 4.9 reshape.246
  747.0 3.0 copy.43
  749.9 2.3 gather_fusion.3
  752.2 2.6 gather.19
  754.8 0.0 copy-done.6
  754.8 2.8 fusion.16
  (13 shorter events, 0.1 us)
Async XLA Ops:
  18.2 17.2 %all-to-all-start = ((bf16[8,1,96]{2,1,0:T(2,128)(2,1)}), bf16[8,1,96]{2,1,0:T(2,128)(2,1)S(1)}, u32[]{:S(2)}, u32[]{:S(2)}) async-start(bf16[8,1,96]{2,1,0:T(2,128)(2,1)} %all_to_all.16), calls=%async_computation | async-start | bytes 8192 | tf_op jit(solution)/shard_map/all_to_all | solution.py:49
  35.5 241.4 %all-to-all-start.2 = ((bf16[8,96,7168]{2,1,0:T(8,128)(2,1)}), bf16[8,96,7168]{2,1,0:T(8,128)(2,1)}, u32[]{:S(2)}, u32[]{:S(2)}) async-start(bf16[8,96,7168]{2,1,0:T(8,128)(2,1)} %bitcast.65), calls=%async_computation.2 | async-start | bytes 22020096 | tf_op jit(solution)/shard_map/all_to_all | solution.py:47
  276.9 243.2 %all-to-all-start.1 = ((bf16[8,96,7168]{2,1,0:T(8,128)(2,1)}), bf16[8,96,7168]{2,1,0:T(8,128)(2,1)}, u32[]{:S(2)}, u32[]{:S(2)}) async-start(bf16[8,96,7168]{2,1,0:T(8,128)(2,1)} %bitcast.64), calls=%async_computation.1 | async-start | bytes 22020096 | tf_op jit(solution)/shard_map/all_to_all | solution.py:48
  285.4 362.0 %reduce-scatter.2.cloned.1.call-start = ((), (), s32[]{:S(2)}) async-start(), calls=%async_computation.5 | async-start | bytes 13762560 | tf_op jit(solution)/shard_map/reduce_scatter | solution.py:81
  520.0 7.1 copy-start.1
  527.1 8.3 %copy-start = (bf16[1,7168,256]{2,1,0:T(8,128)(2,1)S(1)}, bf16[1,7168,256]{2,1,0:T(8,128)(2,1)}, u32[]{:S(2)}) copy-start(bf16[1,7168,256]{2,1,0:T(8,128)(2,1)} %param.12) | copy-start | bytes 11010052
  535.5 9.1 %copy-start.4 = (bf16[768,256]{1,0:T(8,128)(2,1)}, bf16[768,256]{1,0:T(8,128)(2,1)S(1)}, u32[]{:S(2)}) copy-start(bf16[768,256]{1,0:T(8,128)(2,1)S(1)} %get-tuple-element.5) | copy-start | bytes 1179652
  535.5 9.1 %copy-start.2 = (bf16[768,256]{1,0:T(8,128)(2,1)}, bf16[768,256]{1,0:T(8,128)(2,1)S(1)}, u32[]{:S(2)}) copy-start(bf16[768,256]{1,0:T(8,128)(2,1)S(1)} %get-tuple-element.4) | copy-start | bytes 1179652
  673.3 11.4 %copy-start.7 = (s32[128,2]{0,1:T(2,128)S(1)}, s32[128,2]{0,1:T(2,128)}, u32[]{:S(2)}) copy-start(s32[128,2]{0,1:T(2,128)} %param.8) | copy-start | bytes 3076
  676.8 65.2 %all-to-all-start.3 = ((bf16[8,2,86016]{2,1,0:T(2,128)(2,1)}), bf16[8,2,86016]{2,1,0:T(2,128)(2,1)S(1)}, u32[]{:S(2)}, u32[]{:S(2)}) async-start(bf16[8,2,86016]{2,1,0:T(2,128)(2,1)} %reshape.245), calls=%async_computation.4 | async-start | bytes 5505024 | tf_op jit(solution)/shard_map/all_to_all | solution.py:84
  686.6 9.5 %copy-start.3 = (bf16[768,256]{1,0:T(8,128)(2,1)S(1)}, bf16[768,256]{1,0:T(8,128)(2,1)}, u32[]{:S(2)}) copy-start(bf16[768,256]{1,0:T(8,128)(2,1)} %copy-done.2) | copy-start | bytes 1179652
  696.1 9.1 %copy-start.5 = (bf16[768,256]{1,0:T(8,128)(2,1)S(1)}, bf16[768,256]{1,0:T(8,128)(2,1)}, u32[]{:S(2)}) copy-start(bf16[768,256]{1,0:T(8,128)(2,1)} %copy-done.4) | copy-start | bytes 1179652
  746.9 7.8 %copy-start.6 = (pred[128,2]{1,0:T(8,128)(4,1)S(1)}, pred[128,2]{1,0:T(8,128)(4,1)}, u32[]{:S(2)}) copy-start(pred[128,2]{1,0:T(8,128)(4,1)} %copy.33) | copy-start | bytes 772
Sparse Core Ops, SparseCore 0:
  557.2 90.1 reduce-scatter.1
where the time goes:
time: 776 us; the launch traced here: 765 us
  waiting for transfers between devices  569 us (73%)
  matrix products  71.5 us (9%)
  local copies, waits for them, and re-layouts  60.1 us (8%)
  starting transfers between devices  27.4 us (4%)
  other arithmetic  21.8 us (3%)
  between operations  14.5 us (2%)
    all_to_all x1, waiting for transfers between devices, per_device(): lax.all_to_all(back_send, 'expert', split_axis=0, concat_axis=1, tiled=True)  227 us
    all_to_all x1, waiting for transfers between devices, per_device(): lax.all_to_all(token_send, 'expert', split_axis=0, concat_axis=1, tiled=T...  224 us
    reduce_scatter x1, waiting for transfers between devices, per_device(): lax.psum_scatter((up_term + gate_term).astype(jnp.bfloat16), 'dp', scatte...  90.3 us
    all_to_all x1, waiting for transfers between devices, per_device(): lax.all_to_all(slot_back, 'expert', split_axis=2, concat_axis=1, tiled=True)  27.7 us
    gather x2, local copies, waits for them, and re-layouts, pad_rows(): return extended[owners // top_count]  18.9 us
    unnamed x1, other arithmetic  17 us
  transfers between devices with their start and end apart: 5, of which 4 were waited for; matrix products, arithmetic and copies ran while one was open for 8% of the time, Pallas kernels for 0%

commit v1 on v0

--- a/solution.py
+++ b/solution.py
@@ -28,7 +28,7 @@
     return extended[owners // top_count]
 
 
-def per_device(tokens, routes, route_gates, cotangent, weight_gate, weight_up, weight_down):
+def per_device_slots(tokens, routes, route_gates, cotangent, weight_gate, weight_up, weight_down):
     members = lax.axis_size("expert")
     groups = lax.axis_size("dp")
     local_experts = weight_gate.shape[0]
@@ -92,6 +92,58 @@
     return (grad_tokens, grad_gate, grad_up, grad_down)
 
 
+def dot(a, b, dims):
+    return lax.dot_general(a, b, (dims, ((), ())), preferred_element_type=jnp.float32)
+
+
+def per_device_dense(tokens, routes, route_gates, cotangent, weight_gate, weight_up, weight_down):
+    members = lax.axis_size("expert")
+    groups = lax.axis_size("dp")
+    me = lax.axis_index("expert")
+    part = lax.axis_index("dp")
+    rows, width = tokens.shape
+    quarter = width // groups
+    w_gate, w_up, w_down = weight_gate[0], weight_up[0], weight_down[0]
+
+    def spread(x):
+        mine = lax.dynamic_slice_in_dim(x, part * quarter, quarter, 1)
+        whole = lax.all_gather(mine, ("dp", "expert"), axis=0, tiled=True)
+        return whole.reshape(groups, members * rows, quarter)
+
+    owned = (routes[:, :, None] == jnp.arange(members, dtype=routes.dtype)).astype(jnp.float32)
+    weight_of = jnp.sum(owned * route_gates.astype(jnp.float32)[:, :, None], axis=1)
+    weight_all = lax.all_gather(weight_of, "expert", axis=0, tiled=True)
+    scale = lax.dynamic_slice_in_dim(weight_all, me, 1, 1)
+
+    tok, cot = spread(tokens), spread(cotangent)
+    blocks = [slice(i * quarter, (i + 1) * quarter) for i in range(groups)]
+    pre_gate = sum(dot(tok[i], w_gate[s], ((1,), (0,))) for i, s in enumerate(blocks))
+    pre_up = sum(dot(tok[i], w_up[s], ((1,), (0,))) for i, s in enumerate(blocks))
+    sigma = jax.nn.sigmoid(pre_gate)
+    activated = pre_gate * sigma
+    scaled_hidden = (scale * activated * pre_up).astype(jnp.bfloat16)
+    back_hidden = scale * sum(dot(cot[i], w_down[:, s], ((1,), (1,))) for i, s in enumerate(blocks))
+    back_up = (back_hidden * activated).astype(jnp.bfloat16)
+    back_gate = (back_hidden * pre_up * sigma * (1.0 + pre_gate * (1.0 - sigma))).astype(
+        jnp.bfloat16
+    )
+    term = dot(back_up, w_up, ((1,), (1,))) + dot(back_gate, w_gate, ((1,), (1,)))
+    part_sum = lax.psum_scatter(
+        term.astype(jnp.bfloat16), "dp", scatter_dimension=1, tiled=True
+    )
+    grad_tokens = lax.psum_scatter(part_sum, "expert", scatter_dimension=0, tiled=True)
+    grad_gate = jnp.concatenate(
+        [dot(tok[i], back_gate, ((0,), (0,))).astype(jnp.bfloat16) for i in range(groups)], 0
+    )
+    grad_up = jnp.concatenate(
+        [dot(tok[i], back_up, ((0,), (0,))).astype(jnp.bfloat16) for i in range(groups)], 0
+    )
+    grad_down = jnp.concatenate(
+        [dot(scaled_hidden, cot[i], ((0,), (0,))).astype(jnp.bfloat16) for i in range(groups)], 1
+    )
+    return (grad_tokens, grad_gate[None], grad_up[None], grad_down[None])
+
+
 def solution(mesh):
     placed = (
         P("expert", None),
@@ -103,7 +155,7 @@
         P("expert", "dp", None),
     )
     return jax.shard_map(
-        per_device,
+        per_device_dense if mesh.shape["expert"] <= 8 else per_device_slots,
         mesh=mesh,
         in_specs=placed,
         out_specs=(

time: 776 us -> 480 us (0.62); the launches traced: 765 us -> 477 us
  waiting for transfers between devices: 569 us -> 342 us
  local copies, waits for them, and re-layouts: 60.1 us -> 6.27 us
  starting transfers between devices: 27.4 us -> 0.16 us
  blocking collectives: 0 us -> 26 us
  other arithmetic: 21.8 us -> 6.67 us
  matrix products: 71.5 us -> 82.6 us
    all_to_all x4 -> x0, waiting for transfers between devices: 479 us -> none  [the longest x1 227 us: per_device(): lax.all_to_all(back_send, 'expert', split_axis=0, concat_axis=1, tiled=True)]
    all_gather x0 -> x2, waiting for transfers between devices: none -> 175 us  [spread(): whole = lax.all_gather(mine, ('dp', 'expert'), axis=0, tiled=True)]
    reduce_scatter x1 -> x2, waiting for transfers between devices: 90.3 us -> 166 us  [the longest x1 111 us: per_device_dense(): lax.psum_scatter(term.astype(jnp.bfloat16), 'dp', scatter_dimension=1, ti...]
    gather x5 -> x0, local copies, waits for them, and re-layouts: 28.7 us -> none  [the longest x2 18.9 us: pad_rows(): return extended[owners // top_count]]
    all_to_all x4 -> x0, starting transfers between devices: 26.9 us -> none  [the longest x1 8.49 us: per_device(): lax.all_to_all(back_send, 'expert', split_axis=0, concat_axis=1, tiled=True)]
    all_gather x0 -> x1, blocking collectives: none -> 26 us  [per_device_dense(): weight_all = lax.all_gather(weight_of, 'expert', axis=0, tiled=True)]
    unnamed x1, other arithmetic: 17 us -> 0.01 us
    dot_general x8 -> x26, matrix products: 71.5 us -> 82.6 us  [dot(): lax.dot_general(a, b, (dims, ((), ())), preferred_element_type=jnp.float32)]
  transfers between devices with their start and end apart: 5 -> 4, of which waited for: 4 -> 4; matrix products, arithmetic and copies ran while one was open for 8% -> 9% of each run, Pallas kernels for 0% -> 0%
where the time goes in v1:
time: 480 us; the launch traced here: 477 us
  waiting for transfers between devices  342 us (71%)
  matrix products  82.6 us (17%)
  blocking collectives  26 us (5%)
  between operations  14 us (3%)
  other arithmetic  6.67 us (1%)
  local copies, waits for them, and re-layouts  6.27 us (1%)
    all_gather x2, waiting for transfers between devices, spread(): whole = lax.all_gather(mine, ('dp', 'expert'), axis=0, tiled=True)  175 us
    reduce_scatter x1, waiting for transfers between devices, per_device_dense(): lax.psum_scatter(term.astype(jnp.bfloat16), 'dp', scatter_dimension=1, ti...  111 us
    dot_general x26, matrix products, dot(): lax.dot_general(a, b, (dims, ((), ())), preferred_element_type=jnp.float32)  82.6 us
    reduce_scatter x1, waiting for transfers between devices, per_device_dense(): lax.psum_scatter(part_sum, 'expert', scatter_dimension=0, tiled=True)  55.3 us
    all_gather x1, blocking collectives, per_device_dense(): weight_all = lax.all_gather(weight_of, 'expert', axis=0, tiled=True)  26 us
  transfers between devices with their start and end apart: 4, of which 4 were waited for; matrix products, arithmetic and copies ran while one was open for 9% of the time, Pallas kernels for 0%

profile of v1, /device:TPU:20, one launch (start us, length us, event | category | flops | bytes accessed | tf_op | source)
XLA Modules:
  0.0 477.4 jit_solution(11515466983095703424)
XLA Ops:
  7.2 0.0 copy-start
  7.2 0.0 all-gather.3.cloned.1.call-start
  7.2 1.4 copy-done
  8.7 0.8 constant_dynamic-slice_fusion.1
  9.5 0.0 all-gather.3.cloned.1.call-update
  9.5 0.0 all-gather.5.cloned.1.call-start
  9.5 1.8 constant_dynamic-slice_fusion
  11.4 0.0 all-gather.5.cloned.1.call-update
  11.4 0.0 reduce-scatter.3.cloned.1.call-start
  11.4 0.7 convert_element_type.52
  12.1 0.7 select_reduce_fusion
  12.8 26.0 %all_gather.9 = f32[1024,8]{0,1:T(8,128)S(1)} all-gather(f32[128,8]{0,1:T(8,128)S(1)} %select_reduce_fusion), channel_id=1, replica_groups=mesh['expert'=8,'dp'=4] {'expert'}, dimensions={0}, use_global_device_ids=true | all-gather | bytes 36864 | tf_op jit(solution)/shard_map/all_gather | solution.py:115
  38.8 78.2 %all-gather.3.cloned.1.call-done = bf16[4096,1792]{1,0:T(8,128)(2,1)} async-done(((bf16[128,1792]{1,0:T(8,128)(2,1)}), bf16[4096,1792]{1,0:T(8,128)(2,1)}) %all-gather.3.cloned.1.call-update) | async-done | bytes 14680080 | tf_op jit(solution)/shard_map/all_gather | solution.py:110
  117.1 0.0 copy-start.5
  117.1 3.6 fusion.13
  120.7 0.0 copy-done.5
  120.7 3.2 fusion.73
  123.9 3.2 fusion.76
  127.1 97.0 %all-gather.5.cloned.1.call-done = bf16[4096,1792]{1,0:T(8,128)(2,1)} async-done(((bf16[128,1792]{1,0:T(8,128)(2,1)}), bf16[4096,1792]{1,0:T(8,128)(2,1)}) %all-gather.5.cloned.1.call-update) | async-done | bytes 14680080 | tf_op jit(solution)/shard_map/all_gather | solution.py:110
  224.1 0.0 copy-start.2
  224.1 0.0 copy-start.4
  224.1 3.6 fusion.45
  227.6 0.0 copy-done.2
  227.6 4.0 fusion.58
  231.6 1.2 copy-done.4
  232.8 0.0 copy-start.3
  232.8 1.1 fusion.64
  234.0 0.9 copy-done.3
  234.9 1.1 fusion.47
  236.0 1.1 fusion.55
  237.1 1.1 fusion.61
  238.2 1.1 fusion.67
  239.4 3.4 fusion.82
  242.8 1.5 multiply_convert_fusion
  244.3 12.1 %fusion.1 = f32[1024,7168]{1,0:T(8,128)} fusion(bf16[1024,256]{1,0:T(8,128)(2,1)S(1)} %get-tuple-element.6, bf16[1,7168,256]{2,1,0:T(8,128)(2,1)S(1)} %copy-done.2), kind=kOutput, calls=%fused_computation.5 | convolution fusion | flops 3758096384 | bytes 33554432 | tf_op jit(solution)/shard_map/dot_general | solution.py:96
  256.4 18.0 %add_convert_fusion = bf16[1024,7168]{1,0:T(8,128)(2,1)} fusion(f32[1024,7168]{1,0:T(8,128)} %fusion.1, bf16[1024,256]{1,0:T(8,128)(2,1)S(1)} %get-tuple-element.5, bf16[1,7168,256]{2,1,0:T(8,128)(2,1)} %param.11), kind=kOutput, calls=%fused_computation | convolution fusion | flops 3772776448 | bytes 48234496 | tf_op jit(solution)/shard_map/dot_general | solution.py:96
  274.3 0.0 reduce-scatter.3.cloned.1.call-update
  274.3 0.0 reduce-scatter.5.cloned.1.call-start
  274.4 111.1 %reduce-scatter.3.cloned.1.call-done = bf16[1024,1792]{1,0:T(8,128)(2,1)} async-done(((bf16[1024,7168]{1,0:T(8,128)(2,1)}), bf16[1024,1792]{1,0:T(8,128)(2,1)}) %reduce-scatter.3.cloned.1.call-update) | async-done | bytes 3670032 | tf_op jit(solution)/shard_map/reduce_scatter | solution.py:131
  385.5 0.0 reduce-scatter.5.cloned.1.call-update
  385.5 3.2 fusion.28
  388.7 3.2 fusion.25
  391.9 0.0 slice-start
  391.9 0.0 slice-start.1
  391.9 3.3 fusion.22
  395.2 0.0 slice-start.2
  395.2 3.4 fusion.19
  398.6 0.0 slice-start.3
  398.6 3.4 convolution_convert_fusion.4
  402.0 0.0 slice-done
  402.0 0.0 slice-done.1
  402.0 0.0 slice-done.2
  402.0 0.0 slice-done.3
  402.0 1.2 convolution_convert_fusion.5
  403.2 1.2 convolution_convert_fusion.6
  404.4 1.2 convolution_convert_fusion.7
  405.5 1.2 convolution_convert_fusion
  406.7 1.2 convolution_convert_fusion.1
  407.9 1.2 convolution_convert_fusion.2
  409.1 1.2 convolution_convert_fusion.3
  410.2 2.0 maximum_bitcast_fusion.2
  412.3 3.3 maximum_bitcast_fusion
  415.6 55.3 %reduce-scatter.5.cloned.1.call-done = bf16[128,1792]{1,0:T(8,128)(2,1)} async-done(((bf16[1024,1792]{1,0:T(8,128)(2,1)}), bf16[128,1792]{1,0:T(8,128)(2,1)}) %reduce-scatter.5.cloned.1.call-update) | async-done | bytes 458768 | tf_op jit(solution)/shard_map/reduce_scatter | solution.py:134
  470.8 0.0 copy-done.1
  (3 shorter events, 0.0 us)
Async XLA Ops:
  7.2 1.5 copy-start
  7.2 109.9 %all-gather.3.cloned.1.call-start = ((), (), s32[]{:S(2)}) async-start(), calls=%async_computation.2 | async-start | bytes 15138816 | tf_op jit(solution)/shard_map/all_gather | solution.py:110
  9.5 214.6 %all-gather.5.cloned.1.call-start = ((), (), s32[]{:S(2)}) async-start(), calls=%async_computation.3 | async-start | bytes 15138816 | tf_op jit(solution)/shard_map/all_gather | solution.py:110
  11.4 374.1 %reduce-scatter.3.cloned.1.call-start = ((), (), s32[]{:S(2)}) async-start(), calls=%async_computation.4 | async-start | bytes 18350080 | tf_op jit(solution)/shard_map/reduce_scatter | solution.py:131
  117.1 3.6 copy-start.5
  224.1 3.6 copy-start.2
  224.1 8.8 %copy-start.4 = (bf16[4096,1792]{1,0:T(8,128)(2,1)S(1)}, bf16[4096,1792]{1,0:T(8,128)(2,1)}, u32[]{:S(2)}) copy-start(bf16[4096,1792]{1,0:T(8,128)(2,1)} %all-gather.5.cloned.1.call-done) | copy-start | bytes 44040196
  232.8 2.0 copy-start.3
  274.3 196.5 %reduce-scatter.5.cloned.1.call-start = ((), (), s32[]{:S(2)}) async-start(), calls=%async_computation.5 | async-start | bytes 4128768 | tf_op jit(solution)/shard_map/reduce_scatter | solution.py:134
  391.9 10.1 %slice-start = ((s8[14680064]{0:T(1024)(128)(4,1)}), s8[4194304]{0:T(1024)(128)(4,1)S(1)}, s32[]{:S(2)}) async-start(s8[14680064]{0:T(1024)(128)(4,1)} %bitcast.56), calls=%async_computation.6 | async-start | bytes 8388608
  391.9 10.1 %slice-start.1 = ((s8[14680064]{0:T(1024)(128)(4,1)}), s8[4194304]{0:T(1024)(128)(4,1)S(1)}, s32[]{:S(2)}) async-start(s8[14680064]{0:T(1024)(128)(4,1)} %bitcast.56), calls=%async_computation.7 | async-start | bytes 8388608
  395.2 6.8 %slice-start.2 = ((s8[14680064]{0:T(1024)(128)(4,1)}), s8[4194304]{0:T(1024)(128)(4,1)S(1)}, s32[]{:S(2)}) async-start(s8[14680064]{0:T(1024)(128)(4,1)} %bitcast.56), calls=%async_computation.8 | async-start | bytes 8388608
  398.6 3.4 slice-start.3
  412.3 58.6 %copy-start.1 = (bf16[128,7168]{1,0:T(8,128)(2,1)S(1)}, bf16[128,7168]{1,0:T(8,128)(2,1)}, u32[]{:S(2)}) copy-start(bf16[128,7168]{1,0:T(8,128)(2,1)} %param.10) | copy-start | bytes 5505028
Sparse Core Ops, SparseCore 0:
  11.4 105.5 all-gather.2
  120.5 103.5 all-gather.4
  274.5 110.9 reduce-scatter.2
  389.6 81.2 reduce-scatter.4

commit v2 on v0

--- a/solution.py
+++ b/solution.py
@@ -1,6 +1,8 @@
 import jax
 import jax.numpy as jnp
 from jax import lax
+from jax.experimental import pallas as pl
+from jax.experimental.pallas import tpu as pltpu
 from jax.sharding import PartitionSpec as P
 
 
@@ -28,7 +30,7 @@
     return extended[owners // top_count]
 
 
-def per_device(tokens, routes, route_gates, cotangent, weight_gate, weight_up, weight_down):
+def per_device_slots(tokens, routes, route_gates, cotangent, weight_gate, weight_up, weight_down):
     members = lax.axis_size("expert")
     groups = lax.axis_size("dp")
     local_experts = weight_gate.shape[0]
@@ -92,6 +94,215 @@
     return (grad_tokens, grad_gate, grad_up, grad_down)
 
 
+def dot(a, b, dims):
+    return lax.dot_general(a, b, (dims, ((), ())), preferred_element_type=jnp.float32)
+
+
+MESH = pl.DeviceIdType.MESH
+COLUMNS = 2
+TILE = 8
+
+
+def gather_events(depth):
+    events = []
+    for k in range(1, depth + 1):
+        if k < depth:
+            events += [(-k, 0), (k, 0)]
+        events += [(0, 1)] if k == 1 else [(1 - k, 1), (k - 1, 1)]
+    return events
+
+
+def gather_kernel(depth, held, *refs):
+    ins, outs = refs[:3], refs[3:6]
+    got, sent, local = refs[6:]
+    e, d = lax.axis_index("expert"), lax.axis_index("dp")
+    z, x, y, c = e // COLUMNS, e % COLUMNS, d // 2, d % 2
+    half = held // 2
+    across = 3 * half // 8
+    plane = half - across
+
+    spots = {
+        "up": (e + COLUMNS, d),
+        "down": (e - COLUMNS, d),
+        "x": (z * COLUMNS + 1 - x, d),
+        "y": (e, (1 - y) * 2 + c),
+        "core": (e, y * 2 + 1 - c),
+    }
+    have = {"up": z + 1 < depth, "down": z > 0}
+
+    barrier = pltpu.get_barrier_semaphore()
+    for name, spot in spots.items():
+        def greet(spot=spot):
+            pl.semaphore_signal(barrier, inc=1, device_id=spot, device_id_type=MESH)
+        if name in have:
+            pl.when(have[name])(greet)
+        else:
+            greet()
+    pl.semaphore_wait(barrier, 3 + (z > 0).astype(jnp.int32) + (z + 1 < depth).astype(jnp.int32))
+
+    def area(kind, mine):
+        if kind == "plane":
+            return c * half + y * across, plane
+        if kind == "y":
+            return c * half + (y if mine else 1 - y) * plane, across
+        if kind == "core plane":
+            return (c if mine else 1 - c) * half + y * across, plane
+        return (c if mine else 1 - c) * half + (1 - y) * plane, across
+
+    kinds = ("plane", "y", "core plane", "core y")
+    lanes = ("up", "down", "x", "y", "core plane", "core y")
+
+    def copy(a, lane, b, own=False, mine=True):
+        kind = lane if lane in kinds else "plane"
+        start, size = area(kind, mine)
+        dst = outs[a].at[pl.ds(b * held + start, size)]
+        src = ins[a].at[pl.ds(start, size)] if own else dst
+        return pltpu.make_async_remote_copy(
+            src_ref=src,
+            dst_ref=dst,
+            send_sem=sent.at[a, lanes.index(lane), b],
+            recv_sem=got.at[a, kinds.index(kind), b],
+            device_id=spots["core" if lane[:4] == "core" else lane],
+            device_id_type=MESH,
+        )
+
+    def arrived(a, kind, b):
+        lane = "x" if kind == "plane" else kind
+        copy(a, lane, b, mine=False).wait_recv()
+
+    def maybe(cond, fn):
+        pl.when(cond)(fn)
+
+    for a in range(3):
+        maybe(have["up"], lambda a=a: copy(a, "up", e, True).start())
+        maybe(have["down"], lambda a=a: copy(a, "down", e, True).start())
+        copy(a, "x", e, True).start()
+    keep = [
+        pltpu.make_async_copy(ins[a], outs[a].at[pl.ds(e * held, held)], local.at[a])
+        for a in range(3)
+    ]
+    for k in keep:
+        k.start()
+
+    events = gather_events(depth)
+
+    def where(event):
+        off, other = event
+        zz = z + off
+        block = zz * COLUMNS + (1 - x if other else x)
+        return (zz >= 0) & (zz < depth), block
+
+    def onward(event):
+        off, other = event
+        if other or off == 0:
+            return None
+        return "up" if off < 0 else "down"
+
+    def plane_event(event):
+        ok, b = where(event)
+        lane = onward(event)
+
+        @pl.when(ok)
+        def _():
+            for a in range(3):
+                arrived(a, "plane", b)
+                if lane:
+                    maybe(have[lane], lambda a=a: copy(a, lane, b).start())
+                    copy(a, "x", b).start()
+                copy(a, "y", b).start()
+                copy(a, "core plane", b).start()
+
+    def y_event(event):
+        ok, b = where(event)
+
+        @pl.when(ok)
+        def _():
+            for a in range(3):
+                arrived(a, "y", b)
+                copy(a, "core y", b).start()
+
+    lag = 3
+    for i, event in enumerate(events):
+        plane_event(event)
+        if i >= lag:
+            y_event(events[i - lag])
+    for event in events[len(events) - lag:]:
+        y_event(event)
+
+    for k in keep:
+        k.wait()
+    for a in range(3):
+        maybe(have["up"], lambda a=a: copy(a, "up", e, True).wait_send())
+        maybe(have["down"], lambda a=a: copy(a, "down", e, True).wait_send())
+        copy(a, "x", e, True).wait_send()
+    for event in events:
+        ok, b = where(event)
+        lane = onward(event)
+
+        @pl.when(ok)
+        def _(b=b, lane=lane):
+            for a in range(3):
+                arrived(a, "core plane", b)
+                arrived(a, "core y", b)
+                if lane:
+                    maybe(have[lane], lambda a=a: copy(a, lane, b).wait_send())
+                    copy(a, "x", b).wait_send()
+                copy(a, "y", b).wait_send()
+                copy(a, "core plane", b).wait_send()
+                copy(a, "core y", b).wait_send()
+
+
+def gather_all(arrays):
+    members = lax.axis_size("expert")
+    held = arrays[0].shape[0] // TILE
+    tiled = [v.reshape(held, TILE, v.shape[1]) for v in arrays]
+    outs = pl.pallas_call(
+        lambda *refs: gather_kernel(members // COLUMNS, held, *refs),
+        out_shape=[
+            jax.ShapeDtypeStruct((members * held, TILE, v.shape[1]), v.dtype) for v in arrays
+        ],
+        in_specs=[pl.BlockSpec(memory_space=pl.ANY)] * 3,
+        out_specs=[pl.BlockSpec(memory_space=pl.ANY)] * 3,
+        scratch_shapes=[
+            pltpu.SemaphoreType.DMA((3, 4, members)),
+            pltpu.SemaphoreType.DMA((3, 6, members)),
+            pltpu.SemaphoreType.DMA((3,)),
+        ],
+        compiler_params=pltpu.CompilerParams(collective_id=0, has_side_effects=True),
+        name="gather_all",
+    )(*tiled)
+    return [v.reshape(v.shape[0] * TILE, v.shape[2]) for v in outs]
+
+
+def per_device_dense(tokens, routes, route_gates, cotangent, weight_gate, weight_up, weight_down):
+    me = lax.axis_index("expert")
+    w_gate, w_up, w_down = weight_gate[0], weight_up[0], weight_down[0]
+
+    owned = (routes[:, :, None] == jnp.arange(128, dtype=routes.dtype)).astype(jnp.float32)
+    weight_of = jnp.sum(owned * route_gates.astype(jnp.float32)[:, :, None], axis=1)
+    tok, cot, weight_all = gather_all([tokens, cotangent, weight_of.astype(jnp.bfloat16)])
+    scale = lax.dynamic_slice_in_dim(weight_all, me, 1, 1).astype(jnp.float32)
+    pre_gate = dot(tok, w_gate, ((1,), (0,)))
+    pre_up = dot(tok, w_up, ((1,), (0,)))
+    sigma = jax.nn.sigmoid(pre_gate)
+    activated = pre_gate * sigma
+    scaled_hidden = (scale * activated * pre_up).astype(jnp.bfloat16)
+    back_hidden = scale * dot(cot, w_down, ((1,), (1,)))
+    back_up = (back_hidden * activated).astype(jnp.bfloat16)
+    back_gate = (back_hidden * pre_up * sigma * (1.0 + pre_gate * (1.0 - sigma))).astype(
+        jnp.bfloat16
+    )
+    term = dot(back_up, w_up, ((1,), (1,))) + dot(back_gate, w_gate, ((1,), (1,)))
+    part_sum = lax.psum_scatter(
+        term.astype(jnp.bfloat16), "dp", scatter_dimension=1, tiled=True
+    )
+    grad_tokens = lax.psum_scatter(part_sum, "expert", scatter_dimension=0, tiled=True)
+    grad_gate = dot(tok, back_gate, ((0,), (0,))).astype(jnp.bfloat16)
+    grad_up = dot(tok, back_up, ((0,), (0,))).astype(jnp.bfloat16)
+    grad_down = dot(scaled_hidden, cot, ((0,), (0,))).astype(jnp.bfloat16)
+    return (grad_tokens, grad_gate[None], grad_up[None], grad_down[None])
+
+
 def solution(mesh):
     placed = (
         P("expert", None),
@@ -103,7 +314,7 @@
         P("expert", "dp", None),
     )
     return jax.shard_map(
-        per_device,
+        per_device_dense if mesh.shape["expert"] <= 8 else per_device_slots,
         mesh=mesh,
         in_specs=placed,
         out_specs=(

time: 776 us -> 402 us (0.52); the launches traced: 765 us -> 400 us
  waiting for transfers between devices: 569 us -> 170 us
  Pallas kernels: 0 us -> 129 us
  local copies, waits for them, and re-layouts: 60.1 us -> 2.87 us
  starting transfers between devices: 27.4 us -> 0.08 us
  other arithmetic: 21.8 us -> 3.19 us
  matrix products: 71.5 us -> 80.9 us
    all_to_all x4 -> x0, waiting for transfers between devices: 479 us -> none  [the longest x1 227 us: per_device(): lax.all_to_all(back_send, 'expert', split_axis=0, concat_axis=1, tiled=True)]
    pallas_call x0 -> x1, Pallas kernels: none -> 129 us  [gather_all(): pl.pallas_call(lambda *refs: gather_kernel(members // COLUMNS, held, *ref...]
    reduce_scatter x1 -> x2, waiting for transfers between devices: 90.3 us -> 170 us  [the longest x1 113 us: per_device_dense(): lax.psum_scatter(term.astype(jnp.bfloat16), 'dp', scatter_dimension=1, ti...]
    gather x5 -> x0, local copies, waits for them, and re-layouts: 28.7 us -> none  [the longest x2 18.9 us: pad_rows(): return extended[owners // top_count]]
    all_to_all x4 -> x0, starting transfers between devices: 26.9 us -> none  [the longest x1 8.49 us: per_device(): lax.all_to_all(back_send, 'expert', split_axis=0, concat_axis=1, tiled=True)]
    unnamed x1 -> x2, other arithmetic: 17 us -> 0.01 us
    dot_general x8, matrix products: 71.5 us -> 80.9 us  [dot(): lax.dot_general(a, b, (dims, ((), ())), preferred_element_type=jnp.float32)]
    reduce_scatter x1 -> x0, local copies, waits for them, and re-layouts: 8.41 us -> none  [per_device(): lax.psum_scatter((up_term + gate_term).astype(jnp.bfloat16), 'dp', scatte...]
  transfers between devices with their start and end apart: 5 -> 2, of which waited for: 4 -> 2; matrix products, arithmetic and copies ran while one was open for 8% -> 7% of each run, Pallas kernels for 0% -> 0%
where the time goes in v2:
time: 402 us; the launch traced here: 400 us
  waiting for transfers between devices  170 us (42%)
  Pallas kernels  129 us (32%)
  matrix products  80.9 us (20%)
  between operations  14.2 us (4%)
    pallas_call x1, Pallas kernels, gather_all(): pl.pallas_call(lambda *refs: gather_kernel(members // COLUMNS, held, *ref...  129 us
    reduce_scatter x1, waiting for transfers between devices, per_device_dense(): lax.psum_scatter(term.astype(jnp.bfloat16), 'dp', scatter_dimension=1, ti...  113 us
    dot_general x8, matrix products, dot(): lax.dot_general(a, b, (dims, ((), ())), preferred_element_type=jnp.float32)  80.9 us
    reduce_scatter x1, waiting for transfers between devices, per_device_dense(): lax.psum_scatter(part_sum, 'expert', scatter_dimension=0, tiled=True)  56.7 us
  transfers between devices with their start and end apart: 2, of which 2 were waited for; matrix products, arithmetic and copies ran while one was open for 7% of the time, Pallas kernels for 0%

profile of v2, /device:TPU:20, one launch (start us, length us, event | category | flops | bytes accessed | tf_op | source)
XLA Modules:
  0.0 399.7 jit_solution(8273014880392620190)
XLA Ops:
  7.2 0.0 reduce-scatter.3.cloned.1.call-start
  7.2 0.7 convert_element_type.33
  7.9 1.4 select_reduce_fusion
  9.3 128.5 %gather_all.1 = (bf16[128,8,7168]{2,1,0:T(8,128)(2,1)}, bf16[128,8,7168]{2,1,0:T(8,128)(2,1)}, bf16[128,8,128]{2,1,0:T(8,128)(2,1)}) custom-call(bf16[16,8,7168]{2,1,0:T(8,128)(2,1)} %bitcast.66, bf16[16,8,7168]{2,1,0:T(8,128)(2,1)} %bitcast.67, bf16[16,8,128]{2,1,0:T(8,128)(2,1)} %bitcast.69), custom_call_target="tpu_custom_call" | custom-call | tf_op jit(solution)/shard_map/gather_all/pallas_call | solution.py:259
  137.9 1.1 dynamic-slice_convert_fusion
  139.0 0.0 slice-start
  139.0 0.2 copy.18
  139.1 0.0 slice-start.1
  139.1 0.0 slice-start.2
  139.2 0.0 slice-start.3
  139.2 0.0 copy-start.7
  139.2 8.7 %fusion.4 = f32[1024,256]{1,0:T(8,128)S(1)} fusion(bf16[128,8,7168]{2,1,0:T(8,128)(2,1)} %get-tuple-element.9, bf16[1,7168,256]{2,1,0:T(8,128)(2,1)} %param.12), kind=kOutput, calls=%fused_computation.5 | convolution fusion | flops 3758096384 | bytes 19398656 | tf_op jit(solution)/shard_map/dot_general | solution.py:98
  147.9 0.0 slice-done
  147.9 0.0 slice-done.1
  147.9 0.4 slice-done.2
  148.3 1.2 slice-done.3
  149.5 1.0 copy-done.7
  150.5 0.0 copy-start.1
  150.5 4.0 fusion.36
  154.5 0.0 copy-done.1
  154.5 0.0 copy-start
  154.5 10.6 %multiply_convert_fusion.1 = (bf16[1024,256]{1,0:T(8,128)(2,1)}, bf16[1024,256]{1,0:T(8,128)(2,1)S(1)}, f32[1024,256]{1,0:T(8,128)}) fusion(f32[1024,256]{1,0:T(8,128)S(1)} %fusion.36, f32[1024,256]{1,0:T(8,128)S(1)} %fusion.4, bf16[1,7168,256]{2,1,0:T(8,128)(2,1)S(1)} %copy-done.1, bf16[128,8,7168]{2,1,0:T(8,128)(2,1)} %get-tuple-element.9), kind=kOutput, calls=%fused_computation.27 | convolution fusion | flops 3761504256 | bytes 22544384 | tf_op jit(solution)/shard_map/dot_general | solution.py:98
  165.1 0.0 copy-start.4
  165.1 0.0 copy-done
  165.1 0.0 copy-start.2
  165.1 11.7 %fusion.31 = f32[1024,7168]{1,0:T(8,128)} fusion(bf16[1024,256]{1,0:T(8,128)(2,1)S(1)} %get-tuple-element.11, bf16[1,7168,256]{2,1,0:T(8,128)(2,1)S(1)} %copy-done), kind=kOutput, calls=%fused_computation.20 | convolution fusion | flops 3758096384 | bytes 33554432 | tf_op jit(solution)/shard_map/dot_general | solution.py:98
  176.8 0.0 copy-done.4
  176.8 0.0 copy-done.2
  176.8 17.1 %add_convert_fusion = bf16[1024,7168]{1,0:T(8,128)(2,1)} fusion(f32[1024,7168]{1,0:T(8,128)} %fusion.31, bf16[1024,256]{1,0:T(8,128)(2,1)} %get-tuple-element.10, bf16[1,7168,256]{2,1,0:T(8,128)(2,1)S(1)} %copy-done.2), kind=kOutput, calls=%fused_computation | convolution fusion | flops 3772776448 | bytes 48234496 | tf_op jit(solution)/shard_map/dot_general | solution.py:98
  193.9 0.0 copy-start.3
  193.9 0.0 reduce-scatter.3.cloned.1.call-update
  194.0 0.0 reduce-scatter.5.cloned.1.call-start
  194.0 113.2 %reduce-scatter.3.cloned.1.call-done = bf16[1024,1792]{1,0:T(8,128)(2,1)} async-done(((bf16[1024,7168]{1,0:T(8,128)(2,1)}), bf16[1024,1792]{1,0:T(8,128)(2,1)}) %reduce-scatter.3.cloned.1.call-update) | async-done | bytes 3670032 | tf_op jit(solution)/shard_map/reduce_scatter | solution.py:296
  307.2 0.0 reduce-scatter.5.cloned.1.call-update
  307.3 0.0 copy-done.3
  307.3 0.0 copy-start.6
  307.3 0.0 slice-start.4
  307.3 0.0 slice-start.5
  307.3 11.4 %fusion.27 = bf16[1,256,7168]{2,1,0:T(8,128)(2,1)} fusion(bf16[128,8,7168]{2,1,0:T(8,128)(2,1)} %get-tuple-element.8, f32[1024,256]{1,0:T(8,128)S(1)} %fusion.4, f32[1024]{0:T(1024)S(1)} %bitcast.71, f32[1024,256]{1,0:T(8,128)S(1)} %copy-done.3), kind=kOutput, calls=%fused_computation.18 | convolution fusion | flops 3761766400 | bytes 20451328 | tf_op jit(solution)/shard_map/dot_general | solution.py:98
  318.7 0.0 copy-done.6
  318.7 0.0 copy-start.5
  318.7 0.0 slice-start.6
  318.7 0.0 slice-start.7
  318.7 11.7 %fusion.24 = bf16[1,7168,256]{2,1,0:T(8,128)(2,1)} fusion(bf16[1024,256]{1,0:T(8,128)(2,1)S(1)} %copy-done.6, bf16[128,8,7168]{2,1,0:T(8,128)(2,1)} %get-tuple-element.9), kind=kOutput, calls=%fused_computation.17 | convolution fusion | flops 3759931392 | bytes 18874368 | tf_op jit(solution)/shard_map/dot_general | solution.py:98
  330.4 0.0 slice-done.4
  330.4 0.0 slice-done.5
  330.4 0.0 copy-done.5
  330.4 0.0 slice-done.6
  330.4 0.0 slice-done.7
  330.4 5.8 %fusion.21 = bf16[1,7168,256]{2,1,0:T(8,128)(2,1)} fusion(bf16[1024,256]{1,0:T(8,128)(2,1)S(1)} %copy-done.5, bf16[128,8,7168]{2,1,0:T(8,128)(2,1)S(1)} %bitcast.73), kind=kOutput, calls=%fused_computation.16 | convolution fusion | flops 3759931392 | bytes 18874368 | tf_op jit(solution)/shard_map/dot_general | solution.py:98
  336.2 56.7 %reduce-scatter.5.cloned.1.call-done = bf16[128,1792]{1,0:T(8,128)(2,1)} async-done(((bf16[1024,1792]{1,0:T(8,128)(2,1)}), bf16[128,1792]{1,0:T(8,128)(2,1)}) %reduce-scatter.5.cloned.1.call-update) | async-done | bytes 458768 | tf_op jit(solution)/shard_map/reduce_scatter | solution.py:299
  (2 shorter events, 0.0 us)
Async XLA Ops:
  7.2 300.1 %reduce-scatter.3.cloned.1.call-start = ((), (), s32[]{:S(2)}) async-start(), calls=%async_computation.2 | async-start | bytes 18350080 | tf_op jit(solution)/shard_map/reduce_scatter | solution.py:296
  139.0 8.9 %slice-start = ((s8[14680064]{0:T(1024)(128)(4,1)}), s8[2097152]{0:T(1024)(128)(4,1)S(1)}, s32[]{:S(2)}) async-start(s8[14680064]{0:T(1024)(128)(4,1)} %bitcast.64), calls=%async_computation.4 | async-start | bytes 4194304
  139.1 8.7 %slice-start.1 = ((s8[14680064]{0:T(1024)(128)(4,1)}), s8[4194304]{0:T(1024)(128)(4,1)S(1)}, s32[]{:S(2)}) async-start(s8[14680064]{0:T(1024)(128)(4,1)} %bitcast.64), calls=%async_computation.5 | async-start | bytes 8388608
  139.1 9.1 %slice-start.2 = ((s8[14680064]{0:T(1024)(128)(4,1)}), s8[4194304]{0:T(1024)(128)(4,1)S(1)}, s32[]{:S(2)}) async-start(s8[14680064]{0:T(1024)(128)(4,1)} %bitcast.64), calls=%async_computation.6 | async-start | bytes 8388608
  139.2 10.3 %slice-start.3 = ((s8[14680064]{0:T(1024)(128)(4,1)}), s8[4194304]{0:T(1024)(128)(4,1)S(1)}, s32[]{:S(2)}) async-start(s8[14680064]{0:T(1024)(128)(4,1)} %bitcast.64), calls=%async_computation.7 | async-start | bytes 8388608
  139.2 11.3 %copy-start.7 = (bf16[1,256,7168]{2,1,0:T(8,128)(2,1)S(1)}, bf16[1,256,7168]{2,1,0:T(8,128)(2,1)}, u32[]{:S(2)}) copy-start(bf16[1,256,7168]{2,1,0:T(8,128)(2,1)} %param.13) | copy-start | bytes 11010052
  150.5 4.0 copy-start.1
  154.5 10.6 %copy-start = (bf16[1,7168,256]{2,1,0:T(8,128)(2,1)S(1)}, bf16[1,7168,256]{2,1,0:T(8,128)(2,1)}, u32[]{:S(2)}) copy-start(bf16[1,7168,256]{2,1,0:T(8,128)(2,1)} %param.12) | copy-start | bytes 11010052
  165.1 11.7 %copy-start.4 = (bf16[1024,256]{1,0:T(8,128)(2,1)}, bf16[1024,256]{1,0:T(8,128)(2,1)S(1)}, u32[]{:S(2)}) copy-start(bf16[1024,256]{1,0:T(8,128)(2,1)S(1)} %get-tuple-element.11) | copy-start | bytes 1572868
  165.1 11.7 %copy-start.2 = (bf16[1,7168,256]{2,1,0:T(8,128)(2,1)S(1)}, bf16[1,7168,256]{2,1,0:T(8,128)(2,1)}, u32[]{:S(2)}) copy-start(bf16[1,7168,256]{2,1,0:T(8,128)(2,1)} %param.11) | copy-start | bytes 11010052
  193.9 113.3 %copy-start.3 = (f32[1024,256]{1,0:T(8,128)S(1)}, f32[1024,256]{1,0:T(8,128)}, u32[]{:S(2)}) copy-start(f32[1024,256]{1,0:T(8,128)} %get-tuple-element.12) | copy-start | bytes 3145732
  194.0 198.9 %reduce-scatter.5.cloned.1.call-start = ((), (), s32[]{:S(2)}) async-start(), calls=%async_computation.3 | async-start | bytes 4128768 | tf_op jit(solution)/shard_map/reduce_scatter | solution.py:299
  307.3 11.5 %copy-start.6 = (bf16[1024,256]{1,0:T(8,128)(2,1)S(1)}, bf16[1024,256]{1,0:T(8,128)(2,1)}, u32[]{:S(2)}) copy-start(bf16[1024,256]{1,0:T(8,128)(2,1)} %get-tuple-element.10) | copy-start | bytes 1572868
  307.3 23.1 %slice-start.4 = ((s8[14680064]{0:T(1024)(128)(4,1)}), s8[2097152]{0:T(1024)(128)(4,1)S(1)}, s32[]{:S(2)}) async-start(s8[14680064]{0:T(1024)(128)(4,1)} %bitcast.72), calls=%async_computation.8 | async-start | bytes 4194304
  307.3 23.1 %slice-start.5 = ((s8[14680064]{0:T(1024)(128)(4,1)}), s8[4194304]{0:T(1024)(128)(4,1)S(1)}, s32[]{:S(2)}) async-start(s8[14680064]{0:T(1024)(128)(4,1)} %bitcast.72), calls=%async_computation.9 | async-start | bytes 8388608
  318.7 11.7 %copy-start.5 = (bf16[1024,256]{1,0:T(8,128)(2,1)S(1)}, bf16[1024,256]{1,0:T(8,128)(2,1)}, u32[]{:S(2)}) copy-start(bf16[1024,256]{1,0:T(8,128)(2,1)} %copy-done.4) | copy-start | bytes 1572868
  318.7 11.7 %slice-start.6 = ((s8[14680064]{0:T(1024)(128)(4,1)}), s8[4194304]{0:T(1024)(128)(4,1)S(1)}, s32[]{:S(2)}) async-start(s8[14680064]{0:T(1024)(128)(4,1)} %bitcast.72), calls=%async_computation.10 | async-start | bytes 8388608
  318.7 11.7 %slice-start.7 = ((s8[14680064]{0:T(1024)(128)(4,1)}), s8[4194304]{0:T(1024)(128)(4,1)S(1)}, s32[]{:S(2)}) async-start(s8[14680064]{0:T(1024)(128)(4,1)} %bitcast.72), calls=%async_computation.11 | async-start | bytes 8388608
Sparse Core Ops, SparseCore 0:
  194.1 113.0 reduce-scatter.2
  311.4 81.4 reduce-scatter.4

commit v3 on v2

--- a/solution.py
+++ b/solution.py
@@ -274,6 +274,214 @@
     return [v.reshape(v.shape[0] * TILE, v.shape[2]) for v in outs]
 
 
+def add_into(ref, other):
+    step = 16
+
+    def body(i, carry):
+        rows = pl.ds(pl.multiple_of(i * step, step), step)
+        total = ref[rows, :].astype(jnp.float32) + other[rows, :].astype(jnp.float32)
+        ref[rows, :] = total.astype(ref.dtype)
+        return carry
+
+    lax.fori_loop(0, ref.shape[0] // step, body, 0)
+
+
+def scatter_kernel(
+    depth, back_up, back_gate, w_up, w_gate, out, part, from_core, y_one, x_one, x_two, y_two,
+    from_below, from_above, sent, got,
+):
+    e, d = lax.axis_index("expert"), lax.axis_index("dp")
+    z, x, y, c = e // COLUMNS, e % COLUMNS, d // 2, d % 2
+    half, quarter = part.shape[-2:]
+    spots = {
+        "up": (e + COLUMNS, d),
+        "down": (e - COLUMNS, d),
+        "x": (z * COLUMNS + 1 - x, d),
+        "y": (e, (1 - y) * 2 + c),
+        "core": (e, y * 2 + 1 - c),
+    }
+    have = {"up": z + 1 < depth, "down": z > 0}
+    barrier = pltpu.get_barrier_semaphore()
+    for name, spot in spots.items():
+        def greet(spot=spot):
+            pl.semaphore_signal(barrier, inc=1, device_id=spot, device_id_type=MESH)
+        if name in have:
+            pl.when(have[name])(greet)
+        else:
+            greet()
+    pl.semaphore_wait(barrier, 3 + (z > 0).astype(jnp.int32) + (z + 1 < depth).astype(jnp.int32))
+
+    def copy(q, n, src, dst, lane):
+        return pltpu.make_async_remote_copy(
+            src_ref=src, dst_ref=dst, send_sem=sent.at[q, n], recv_sem=got.at[q, n],
+            device_id=spots[lane], device_id_type=MESH,
+        )
+
+    def core_copy(q, yy):
+        return copy(q, yy, part.at[q, yy, 1 - c], from_core.at[q, yy], "core")
+
+    def y_one_copy(q):
+        return copy(q, 2, part.at[q, 1 - y, c, 0], y_one.at[q], "y")
+
+    def x_two_copy(q, yy):
+        return copy(q, 3 + yy, part.at[q, yy, c, 1, 1 - x], x_two.at[q, yy], "x")
+
+    def x_one_copy(q):
+        return copy(q, 5, part.at[q, y, c, 0, 1 - x], x_one.at[q], "x")
+
+    def y_two_copy(q):
+        return copy(q, 6, part.at[q, 1 - y, c, 1, x], y_two.at[q], "y")
+
+    def up_copy(q, t):
+        return copy(q, 7 + t, part.at[q, y, c, t, x], from_below.at[q, t], "up")
+
+    def down_copy(q, t):
+        return copy(q, 9 + t, part.at[q, y, c, t, x], from_above.at[q, t], "down")
+
+    tile = 256
+    rows = 4 * half
+
+    def terms(q, yy, cc):
+        def body(n, carry):
+            first = pl.multiple_of((yy * 2 + cc) * quarter + n * tile, tile)
+            nt = (((1,), (1,)), ((), ()))
+            taken = pl.ds(q * rows, rows)
+            term = lax.dot_general(
+                back_up[taken, :], w_up[pl.ds(first, tile), :], nt,
+                preferred_element_type=jnp.float32,
+            ) + lax.dot_general(
+                back_gate[taken, :], w_gate[pl.ds(first, tile), :], nt,
+                preferred_element_type=jnp.float32,
+            )
+            term = term.astype(part.dtype)
+            columns = pl.ds(pl.multiple_of(n * tile, tile), tile)
+            for xx in range(2):
+                for t in range(2):
+                    at = (xx * 2 + t) * half
+                    part[q, yy, cc, t, xx, :, columns] = term[at : at + half]
+            return carry
+
+        lax.fori_loop(0, quarter // tile, body, 0)
+
+    def stage_a(q):
+        for yy in range(2):
+            terms(q, yy, 1 - c)
+            core_copy(q, yy).start()
+        for yy in range(2):
+            terms(q, yy, c)
+
+    def stage_b(q):
+        for yy in range(2):
+            core_copy(q, yy).wait_recv()
+            for t in range(2):
+                for xx in range(2):
+                    add_into(part.at[q, yy, c, t, xx], from_core.at[q, yy, t, xx])
+        y_one_copy(q).start()
+        for yy in range(2):
+            x_two_copy(q, yy).start()
+
+    def stage_c(q):
+        y_one_copy(q).wait_recv()
+        for xx in range(2):
+            add_into(part.at[q, y, c, 0, xx], y_one.at[q, xx])
+        x_one_copy(q).start()
+        for yy in range(2):
+            x_two_copy(q, yy).wait_recv()
+            add_into(part.at[q, yy, c, 1, x], x_two.at[q, yy])
+        y_two_copy(q).start()
+
+    def stage_d(q):
+        x_one_copy(q).wait_recv()
+        add_into(part.at[q, y, c, 0, x], x_one.at[q])
+        y_two_copy(q).wait_recv()
+        add_into(part.at[q, y, c, 1, x], y_two.at[q])
+
+    def below(q):
+        for t in range(2):
+            up_copy(q, t).wait_recv()
+            add_into(part.at[q, y, c, t, x], from_below.at[q, t])
+
+    def above(q):
+        for t in range(2):
+            down_copy(q, t).wait_recv()
+            add_into(part.at[q, y, c, t, x], from_above.at[q, t])
+
+    def stage_e(q):
+        @pl.when(z < q)
+        def _():
+            pl.when(z > 0)(lambda: below(q))
+            for t in range(2):
+                up_copy(q, t).start()
+
+        @pl.when(z > q)
+        def _():
+            pl.when(z + 1 < depth)(lambda: above(q))
+            for t in range(2):
+                down_copy(q, t).start()
+
+    order = []
+    low, high = 0, depth - 1
+    while low <= high:
+        order += [low] if low == high else [low, high]
+        low, high = low + 1, high - 1
+    stages = (stage_a, stage_b, stage_c, stage_d, stage_e)
+    for beat in range(depth + len(stages) - 1):
+        for s, stage in enumerate(stages):
+            if 0 <= beat - s < depth:
+                stage(order[beat - s])
+
+    for q in range(depth):
+        @pl.when(z == q)
+        def _(q=q):
+            pl.when(z > 0)(lambda: below(q))
+            pl.when(z + 1 < depth)(lambda: above(q))
+            for t in range(2):
+                out[pl.ds(t * half, half), :] = part[q, y, c, t, x]
+
+    for q in range(depth):
+        for yy in range(2):
+            core_copy(q, yy).wait_send()
+            x_two_copy(q, yy).wait_send()
+        y_one_copy(q).wait_send()
+        x_one_copy(q).wait_send()
+        y_two_copy(q).wait_send()
+        for t in range(2):
+            pl.when(z < q)(lambda q=q, t=t: up_copy(q, t).wait_send())
+            pl.when(z > q)(lambda q=q, t=t: down_copy(q, t).wait_send())
+
+
+def scatter_sum(back_up, back_gate, w_up, w_gate):
+    members = lax.axis_size("expert")
+    depth = members // COLUMNS
+    rows = back_up.shape[0] // members
+    width = w_up.shape[0]
+    quarter, half = width // 4, rows // 2
+    kind = back_up.dtype
+    whole = pl.BlockSpec(memory_space=pltpu.VMEM)
+    return pl.pallas_call(
+        lambda *refs: scatter_kernel(depth, *refs),
+        out_shape=jax.ShapeDtypeStruct((rows, quarter), kind),
+        in_specs=[whole] * 4,
+        out_specs=whole,
+        scratch_shapes=[
+            pltpu.VMEM((depth, 2, 2, 2, 2, half, quarter), kind),
+            pltpu.VMEM((depth, 2, 2, 2, half, quarter), kind),
+            pltpu.VMEM((depth, 2, half, quarter), kind),
+            pltpu.VMEM((depth, half, quarter), kind),
+            pltpu.VMEM((depth, 2, half, quarter), kind),
+            pltpu.VMEM((depth, half, quarter), kind),
+            pltpu.VMEM((depth, 2, half, quarter), kind),
+            pltpu.VMEM((depth, 2, half, quarter), kind),
+            pltpu.SemaphoreType.DMA((depth, 11)),
+            pltpu.SemaphoreType.DMA((depth, 11)),
+        ],
+        compiler_params=pltpu.CompilerParams(
+            collective_id=1, has_side_effects=True, vmem_limit_bytes=56 * 2**20
+        ),
+        name="scatter_sum",
+    )(back_up, back_gate, w_up, w_gate)
+
+
 def per_device_dense(tokens, routes, route_gates, cotangent, weight_gate, weight_up, weight_down):
     me = lax.axis_index("expert")
     w_gate, w_up, w_down = weight_gate[0], weight_up[0], weight_down[0]
@@ -292,11 +500,7 @@
     back_gate = (back_hidden * pre_up * sigma * (1.0 + pre_gate * (1.0 - sigma))).astype(
         jnp.bfloat16
     )
-    term = dot(back_up, w_up, ((1,), (1,))) + dot(back_gate, w_gate, ((1,), (1,)))
-    part_sum = lax.psum_scatter(
-        term.astype(jnp.bfloat16), "dp", scatter_dimension=1, tiled=True
-    )
-    grad_tokens = lax.psum_scatter(part_sum, "expert", scatter_dimension=0, tiled=True)
+    grad_tokens = scatter_sum(back_up, back_gate, w_up, w_gate)
     grad_gate = dot(tok, back_gate, ((0,), (0,))).astype(jnp.bfloat16)
     grad_up = dot(tok, back_up, ((0,), (0,))).astype(jnp.bfloat16)
     grad_down = dot(scaled_hidden, cot, ((0,), (0,))).astype(jnp.bfloat16)

time: 402 us -> 309 us (0.77)
  waiting for transfers between devices: 170 us -> 0 us
  Pallas kernels: 129 us -> 249 us
  matrix products: 80.9 us -> 53.6 us
  between operations: 14.2 us -> 0.74 us
    reduce_scatter x2 -> x0, waiting for transfers between devices: 170 us -> none  [the longest x1 113 us: per_device_dense(): lax.psum_scatter(term.astype(jnp.bfloat16), 'dp', scatter_dimension=1, ti...]
    pallas_call x0 -> x1, Pallas kernels: none -> 120 us  [scatter_sum(): pl.pallas_call(lambda *refs: scatter_kernel(depth, *refs), out_shape=jax....]
    dot_general x8 -> x6, matrix products: 80.9 us -> 53.6 us  [dot(): lax.dot_general(a, b, (dims, ((), ())), preferred_element_type=jnp.float32)]
  transfers between devices with their start and end apart: 2 -> 0, of which waited for: 2 -> 0; matrix products, arithmetic and copies ran while one was open for 7% -> 0% of each run, Pallas kernels for 0% -> 0%
where the time goes in v3:
time: 309 us
  Pallas kernels  249 us (81%)
  matrix products  53.6 us (17%)
  other arithmetic  3.19 us (1%)
    pallas_call x1, Pallas kernels, gather_all(): pl.pallas_call(lambda *refs: gather_kernel(members // COLUMNS, held, *ref...  129 us
    pallas_call x1, Pallas kernels, scatter_sum(): pl.pallas_call(lambda *refs: scatter_kernel(depth, *refs), out_shape=jax....  120 us
    dot_general x6, matrix products, dot(): lax.dot_general(a, b, (dims, ((), ())), preferred_element_type=jnp.float32)  53.6 us

profile of v3, /device:TPU:20, one launch (start us, length us, event | category | flops | bytes accessed | tf_op | source)
XLA Modules:
  0.0 309.2 jit_solution(2657465513577818465)
XLA Ops:
  0.6 0.7 convert_element_type.30
  1.3 1.4 select_reduce_fusion
  2.7 128.5 %gather_all.1 = (bf16[128,8,7168]{2,1,0:T(8,128)(2,1)}, bf16[128,8,7168]{2,1,0:T(8,128)(2,1)}, bf16[128,8,128]{2,1,0:T(8,128)(2,1)}) custom-call(bf16[16,8,7168]{2,1,0:T(8,128)(2,1)} %bitcast.62, bf16[16,8,7168]{2,1,0:T(8,128)(2,1)} %bitcast.63, bf16[16,8,128]{2,1,0:T(8,128)(2,1)} %bitcast.65), custom_call_target="tpu_custom_call" | custom-call | tf_op jit(solution)/shard_map/gather_all/pallas_call | solution.py:259
  131.3 1.1 dynamic-slice_convert_fusion
  132.4 0.0 slice-start
  132.4 0.2 copy.18
  132.6 0.0 slice-start.1
  132.6 0.0 slice-start.2
  132.6 0.0 slice-start.3
  132.6 8.5 %fusion.4 = f32[1024,256]{1,0:T(8,128)S(1)} fusion(bf16[128,8,7168]{2,1,0:T(8,128)(2,1)} %get-tuple-element.9, bf16[1,7168,256]{2,1,0:T(8,128)(2,1)} %param.12), kind=kOutput, calls=%fused_computation.4 | convolution fusion | flops 3758096384 | bytes 19398656 | tf_op jit(solution)/shard_map/dot_general | solution.py:98
  141.0 0.0 slice-done
  141.0 0.0 slice-done.1
  141.1 0.6 slice-done.2
  141.7 1.2 slice-done.3
  142.9 0.0 copy-start
  142.9 6.2 %fusion.31 = f32[1024,256]{1,0:T(8,128)S(1)} fusion(bf16[1,256,7168]{2,1,0:T(8,128)(2,1)} %param.13, bf16[128,8,7168]{2,1,0:T(8,128)(2,1)S(1)} %bitcast.59, f32[1024]{0:T(1024)S(1)} %bitcast.66), kind=kOutput, calls=%fused_computation.19 | convolution fusion | flops 3758358528 | bytes 19402752 | tf_op jit(solution)/shard_map/dot_general | solution.py:98
  149.1 0.0 copy-done
  149.1 10.4 %multiply_convert_fusion.1 = (bf16[1024,256]{1,0:T(8,128)(2,1)}, bf16[1024,256]{1,0:T(8,128)(2,1)}, f32[1024,256]{1,0:T(8,128)S(1)}) fusion(f32[1024,256]{1,0:T(8,128)S(1)} %fusion.31, f32[1024,256]{1,0:T(8,128)S(1)} %fusion.4, bf16[1,7168,256]{2,1,0:T(8,128)(2,1)S(1)} %copy-done, bf16[128,8,7168]{2,1,0:T(8,128)(2,1)} %get-tuple-element.9), kind=kOutput, calls=%fused_computation.21 | convolution fusion | flops 3761504256 | bytes 22544384 | tf_op jit(solution)/shard_map/dot_general | solution.py:98
  159.5 6.1 %fusion.27 = bf16[1,256,7168]{2,1,0:T(8,128)(2,1)} fusion(bf16[128,8,7168]{2,1,0:T(8,128)(2,1)S(1)} %bitcast.59, f32[1024,256]{1,0:T(8,128)S(1)} %fusion.4, f32[1024]{0:T(1024)S(1)} %bitcast.67, f32[1024,256]{1,0:T(8,128)S(1)} %get-tuple-element.12), kind=kOutput, calls=%fused_computation.17 | convolution fusion | flops 3761766400 | bytes 20451328 | tf_op jit(solution)/shard_map/dot_general | solution.py:98
  165.6 0.0 copy-start.3
  165.6 120.3 %scatter_sum.1 = bf16[128,1792]{1,0:T(8,128)(2,1)} custom-call(bf16[1024,256]{1,0:T(8,128)(2,1)} %get-tuple-element.11.refs_0_, bf16[1024,256]{1,0:T(8,128)(2,1)} %get-tuple-element.10.refs_1_, bf16[7168,256]{1,0:T(8,128)(2,1)} %bitcast.60, bf16[7168,256]{1,0:T(8,128)(2,1)} %bitcast.61), custom_call_target="tpu_custom_call" | custom-call | tf_op jit(solution)/shard_map/scatter_sum/pallas_call | solution.py:461
  285.9 0.0 copy-done.3
  285.9 0.0 copy-start.2
  285.9 11.2 %fusion.24 = bf16[1,7168,256]{2,1,0:T(8,128)(2,1)} fusion(bf16[1024,256]{1,0:T(8,128)(2,1)S(1)} %copy-done.3, bf16[128,8,7168]{2,1,0:T(8,128)(2,1)} %get-tuple-element.9), kind=kOutput, calls=%fused_computation.16 | convolution fusion | flops 3759931392 | bytes 18874368 | tf_op jit(solution)/shard_map/dot_general | solution.py:98
  297.2 0.0 copy-done.2
  297.2 0.0 copy-start.1
  297.2 11.2 %fusion.21 = bf16[1,7168,256]{2,1,0:T(8,128)(2,1)} fusion(bf16[1024,256]{1,0:T(8,128)(2,1)S(1)} %copy-done.2, bf16[128,8,7168]{2,1,0:T(8,128)(2,1)} %get-tuple-element.9), kind=kOutput, calls=%fused_computation.15 | convolution fusion | flops 3759931392 | bytes 18874368 | tf_op jit(solution)/shard_map/dot_general | solution.py:98
  308.4 0.0 copy-done.1
  308.4 0.8 copy.20
  (1 shorter events, 0.0 us)
Async XLA Ops:
  132.4 8.7 %slice-start = ((s8[14680064]{0:T(1024)(128)(4,1)}), s8[2097152]{0:T(1024)(128)(4,1)S(1)}, s32[]{:S(2)}) async-start(s8[14680064]{0:T(1024)(128)(4,1)} %bitcast.58), calls=%async_computation | async-start | bytes 4194304
  132.6 8.5 %slice-start.1 = ((s8[14680064]{0:T(1024)(128)(4,1)}), s8[4194304]{0:T(1024)(128)(4,1)S(1)}, s32[]{:S(2)}) async-start(s8[14680064]{0:T(1024)(128)(4,1)} %bitcast.58), calls=%async_computation.1 | async-start | bytes 8388608
  132.6 9.1 %slice-start.2 = ((s8[14680064]{0:T(1024)(128)(4,1)}), s8[4194304]{0:T(1024)(128)(4,1)S(1)}, s32[]{:S(2)}) async-start(s8[14680064]{0:T(1024)(128)(4,1)} %bitcast.58), calls=%async_computation.2 | async-start | bytes 8388608
  132.6 10.3 %slice-start.3 = ((s8[14680064]{0:T(1024)(128)(4,1)}), s8[4194304]{0:T(1024)(128)(4,1)S(1)}, s32[]{:S(2)}) async-start(s8[14680064]{0:T(1024)(128)(4,1)} %bitcast.58), calls=%async_computation.3 | async-start | bytes 8388608
  142.9 6.2 %copy-start = (bf16[1,7168,256]{2,1,0:T(8,128)(2,1)S(1)}, bf16[1,7168,256]{2,1,0:T(8,128)(2,1)}, u32[]{:S(2)}) copy-start(bf16[1,7168,256]{2,1,0:T(8,128)(2,1)} %param.11) | copy-start | bytes 11010052
  165.6 120.3 %copy-start.3 = (bf16[1024,256]{1,0:T(8,128)(2,1)S(1)}, bf16[1024,256]{1,0:T(8,128)(2,1)}, u32[]{:S(2)}) copy-start(bf16[1024,256]{1,0:T(8,128)(2,1)} %get-tuple-element.10.refs_1_) | copy-start | bytes 1572868
  285.9 11.3 %copy-start.2 = (bf16[1024,256]{1,0:T(8,128)(2,1)S(1)}, bf16[1024,256]{1,0:T(8,128)(2,1)}, u32[]{:S(2)}) copy-start(bf16[1024,256]{1,0:T(8,128)(2,1)} %get-tuple-element.11.refs_0_) | copy-start | bytes 1572868
  297.2 11.2 %copy-start.1 = (bf16[128,1792]{1,0:T(8,128)(2,1)S(1)}, bf16[128,1792]{1,0:T(8,128)(2,1)}, u32[]{:S(2)}) copy-start(bf16[128,1792]{1,0:T(8,128)(2,1)} %scatter_sum.1) | copy-start | bytes 1376260

commit v4 on v3

--- a/solution.py
+++ b/solution.py
@@ -482,6 +482,107 @@
     )(back_up, back_gate, w_up, w_gate)
 
 
+def hidden_kernel(
+    tok, cot, w_gate, w_up, w_down, scale, back_up, back_gate, back_t, hidden_t, gate, up, back
+):
+    step = pl.program_id(0)
+
+    @pl.when(step == 0)
+    def _():
+        gate[...] = jnp.zeros_like(gate)
+        up[...] = jnp.zeros_like(up)
+        back[...] = jnp.zeros_like(back)
+
+    gate[...] += dot(tok[...], w_gate[...], ((1,), (0,)))
+    up[...] += dot(tok[...], w_up[...], ((1,), (0,)))
+    back[...] += dot(cot[...], w_down[...], ((1,), (1,)))
+
+    @pl.when(step == pl.num_programs(0) - 1)
+    def _():
+        size, units = 128, gate.shape[1]
+
+        def body(i, carry):
+            rows = pl.ds(pl.multiple_of(i * size, size), size)
+            pre_gate, pre_up, factor = gate[rows, :], up[rows, :], scale[rows, :]
+            sigma = jax.nn.sigmoid(pre_gate)
+            activated = pre_gate * sigma
+            back_hidden = factor * back[rows, :]
+            hidden = (factor * activated * pre_up).astype(jnp.bfloat16)
+            down_up = (back_hidden * activated).astype(jnp.bfloat16)
+            down_gate = (
+                back_hidden * pre_up * sigma * (1.0 + pre_gate * (1.0 - sigma))
+            ).astype(jnp.bfloat16)
+            back_up[rows, :] = down_up
+            back_gate[rows, :] = down_gate
+            hidden_t[:, rows] = hidden.T
+            back_t[:units, rows] = down_gate.T
+            back_t[units:, rows] = down_up.T
+            return carry
+
+        lax.fori_loop(0, gate.shape[0] // size, body, 0)
+
+
+def hidden_grads(tok, cot, w_gate, w_up, w_down, scale):
+    rows, width = tok.shape
+    units = w_gate.shape[1]
+    tile = 512
+    kind = tok.dtype
+    across = pl.BlockSpec((rows, tile), lambda i: (0, i))
+    along = pl.BlockSpec((tile, units), lambda i: (i, 0))
+
+    def fixed(shape):
+        return pl.BlockSpec(shape, lambda i: (0, 0))
+
+    shapes = [(rows, units), (rows, units), (2 * units, rows), (units, rows)]
+    return pl.pallas_call(
+        hidden_kernel,
+        grid=(width // tile,),
+        out_shape=[jax.ShapeDtypeStruct(s, kind) for s in shapes],
+        in_specs=[
+            across, across, along, along, pl.BlockSpec((units, tile), lambda i: (0, i)),
+            fixed((rows, 1)),
+        ],
+        out_specs=[fixed(s) for s in shapes],
+        scratch_shapes=[pltpu.VMEM((rows, units), jnp.float32)] * 3,
+        compiler_params=pltpu.CompilerParams(vmem_limit_bytes=40 * 2**20),
+        name="hidden_grads",
+    )(tok, cot, w_gate, w_up, w_down, scale)
+
+
+def weight_kernel(tok, cot, back_t, hidden_t, grad_gate, grad_up, grad_down):
+    units = hidden_t.shape[0]
+    both = dot(back_t[...], tok[...], ((1,), (0,))).astype(grad_gate.dtype)
+    grad_gate[...] = both[:units].T
+    grad_up[...] = both[units:].T
+    grad_down[...] = dot(hidden_t[...], cot[...], ((1,), (0,))).astype(grad_down.dtype)
+
+
+def weight_grads(tok, cot, back_t, hidden_t):
+    rows, width = tok.shape
+    units = hidden_t.shape[0]
+    tile = 512
+    kind = tok.dtype
+    across = pl.BlockSpec((rows, tile), lambda i: (0, i))
+    along = pl.BlockSpec((tile, units), lambda i: (i, 0))
+    return pl.pallas_call(
+        weight_kernel,
+        grid=(width // tile,),
+        out_shape=[
+            jax.ShapeDtypeStruct((width, units), kind),
+            jax.ShapeDtypeStruct((width, units), kind),
+            jax.ShapeDtypeStruct((units, width), kind),
+        ],
+        in_specs=[
+            across, across,
+            pl.BlockSpec((2 * units, rows), lambda i: (0, 0)),
+            pl.BlockSpec((units, rows), lambda i: (0, 0)),
+        ],
+        out_specs=[along, along, pl.BlockSpec((units, tile), lambda i: (0, i))],
+        compiler_params=pltpu.CompilerParams(vmem_limit_bytes=40 * 2**20),
+        name="weight_grads",
+    )(tok, cot, back_t, hidden_t)
+
+
 def per_device_dense(tokens, routes, route_gates, cotangent, weight_gate, weight_up, weight_down):
     me = lax.axis_index("expert")
     w_gate, w_up, w_down = weight_gate[0], weight_up[0], weight_down[0]
@@ -490,20 +591,9 @@
     weight_of = jnp.sum(owned * route_gates.astype(jnp.float32)[:, :, None], axis=1)
     tok, cot, weight_all = gather_all([tokens, cotangent, weight_of.astype(jnp.bfloat16)])
     scale = lax.dynamic_slice_in_dim(weight_all, me, 1, 1).astype(jnp.float32)
-    pre_gate = dot(tok, w_gate, ((1,), (0,)))
-    pre_up = dot(tok, w_up, ((1,), (0,)))
-    sigma = jax.nn.sigmoid(pre_gate)
-    activated = pre_gate * sigma
-    scaled_hidden = (scale * activated * pre_up).astype(jnp.bfloat16)
-    back_hidden = scale * dot(cot, w_down, ((1,), (1,)))
-    back_up = (back_hidden * activated).astype(jnp.bfloat16)
-    back_gate = (back_hidden * pre_up * sigma * (1.0 + pre_gate * (1.0 - sigma))).astype(
-        jnp.bfloat16
-    )
+    back_up, back_gate, back_t, hidden_t = hidden_grads(tok, cot, w_gate, w_up, w_down, scale)
     grad_tokens = scatter_sum(back_up, back_gate, w_up, w_gate)
-    grad_gate = dot(tok, back_gate, ((0,), (0,))).astype(jnp.bfloat16)
-    grad_up = dot(tok, back_up, ((0,), (0,))).astype(jnp.bfloat16)
-    grad_down = dot(scaled_hidden, cot, ((0,), (0,))).astype(jnp.bfloat16)
+    grad_gate, grad_up, grad_down = weight_grads(tok, cot, back_t, hidden_t)
     return (grad_tokens, grad_gate[None], grad_up[None], grad_down[None])
 
 

time: 309 us -> 305 us (0.987)
  matrix products: 53.6 us -> 0 us
  Pallas kernels: 249 us -> 291 us
  local copies, waits for them, and re-layouts: 2.79 us -> 8.46 us
    dot_general x6 -> x0, matrix products: 53.6 us -> none  [dot(): lax.dot_general(a, b, (dims, ((), ())), preferred_element_type=jnp.float32)]
    pallas_call x0 -> x2, Pallas kernels: none -> 42.6 us  [the longest x1 21.4 us: weight_grads(): pl.pallas_call(weight_kernel, grid=(width // tile,), out_shape=[jax.Shape...]
    unnamed x18 -> x13, local copies, waits for them, and re-layouts: 2.79 us -> 8.46 us
where the time goes in v4:
time: 305 us; the launch traced here: 304 us
  Pallas kernels  291 us (95%)
  local copies, waits for them, and re-layouts  8.46 us (3%)
  other arithmetic  3.18 us (1%)
    pallas_call x1, Pallas kernels, gather_all(): pl.pallas_call(lambda *refs: gather_kernel(members // COLUMNS, held, *ref...  129 us
    pallas_call x1, Pallas kernels, scatter_sum(): pl.pallas_call(lambda *refs: scatter_kernel(depth, *refs), out_shape=jax....  120 us
    pallas_call x1, Pallas kernels, weight_grads(): pl.pallas_call(weight_kernel, grid=(width // tile,), out_shape=[jax.Shape...  21.4 us
    pallas_call x1, Pallas kernels, hidden_grads(): pl.pallas_call(hidden_kernel, grid=(width // tile,), out_shape=[jax.Shape...  21.3 us
    unnamed x13, local copies, waits for them, and re-layouts  8.46 us

profile of v4, /device:TPU:20, one launch (start us, length us, event | category | flops | bytes accessed | tf_op | source)
XLA Modules:
  0.0 303.8 jit_solution(3309806856971233517)
XLA Ops:
  0.6 0.7 convert_element_type.14
  1.3 1.4 select_reduce_fusion
  2.7 128.5 %gather_all.1 = (bf16[128,8,7168]{2,1,0:T(8,128)(2,1)}, bf16[128,8,7168]{2,1,0:T(8,128)(2,1)}, bf16[128,8,128]{2,1,0:T(8,128)(2,1)}) custom-call(bf16[16,8,7168]{2,1,0:T(8,128)(2,1)} %bitcast.23, bf16[16,8,7168]{2,1,0:T(8,128)(2,1)} %bitcast.24, bf16[16,8,128]{2,1,0:T(8,128)(2,1)} %bitcast.26), custom_call_target="tpu_custom_call" | custom-call | tf_op jit(solution)/shard_map/gather_all/pallas_call | solution.py:259
  131.3 1.1 dynamic-slice_convert_fusion.scale
  132.4 0.0 copy-start
  132.4 2.0 copy-done
  134.4 0.0 copy-start.1
  134.4 2.0 copy-done.1
  136.5 0.0 copy-start.2
  136.5 2.0 copy-done.2
  138.5 21.3 %hidden_grads.1 = (bf16[1024,256]{1,0:T(8,128)(2,1)S(1)}, bf16[1024,256]{1,0:T(8,128)(2,1)S(1)}, bf16[512,1024]{1,0:T(8,128)(2,1)S(1)}, bf16[256,1024]{1,0:T(8,128)(2,1)S(1)}) custom-call(bf16[1024,7168]{1,0:T(8,128)(2,1)} %bitcast.19, bf16[1024,7168]{1,0:T(8,128)(2,1)} %bitcast.21, bf16[7168,256]{1,0:T(8,128)(2,1)S(1)} %bitcast.15, ...), custom_call_target="tpu_custom_call" | custom-call | tf_op jit(solution)/shard_map/hidden_grads/pallas_call | solution.py:537
  159.8 0.0 copy-start.3
  159.8 0.8 copy-done.3
  160.5 0.0 copy-start.4
  160.5 0.8 copy-done.4
  161.3 120.3 %scatter_sum.1 = bf16[128,1792]{1,0:T(8,128)(2,1)} custom-call(bf16[1024,256]{1,0:T(8,128)(2,1)} %copy-done.3, bf16[1024,256]{1,0:T(8,128)(2,1)} %copy-done.4, bf16[7168,256]{1,0:T(8,128)(2,1)} %bitcast.16, bf16[7168,256]{1,0:T(8,128)(2,1)} %bitcast.14), custom_call_target="tpu_custom_call" | custom-call | tf_op jit(solution)/shard_map/scatter_sum/pallas_call | solution.py:461
  281.6 0.0 copy-start.5
  281.6 21.4 %weight_grads.1 = (bf16[7168,256]{1,0:T(8,128)(2,1)}, bf16[7168,256]{1,0:T(8,128)(2,1)}, bf16[256,7168]{1,0:T(8,128)(2,1)}) custom-call(bf16[1024,7168]{1,0:T(8,128)(2,1)} %bitcast.20, bf16[1024,7168]{1,0:T(8,128)(2,1)} %bitcast.22, bf16[512,1024]{1,0:T(8,128)(2,1)S(1)} %get-tuple-element.19.back_t, bf16[256,1024]{1,0:T(8,128)(2,1)S(1)} %get-tuple-element.20.hidden_t), custom_call_target="tpu_custom_call" | custom-call | tf_op jit(solution)/shard_map/weight_grads/pallas_call | solution.py:567
  303.0 0.0 copy-done.5
  303.0 0.8 copy.14
Async XLA Ops:
  132.4 2.0 copy-start
  134.4 2.0 copy-start.1
  136.5 2.0 copy-start.2
  159.8 0.8 copy-start.3
  160.5 0.8 copy-start.4
  281.6 21.4 %copy-start.5 = (bf16[128,1792]{1,0:T(8,128)(2,1)S(1)}, bf16[128,1792]{1,0:T(8,128)(2,1)}, u32[]{:S(2)}) copy-start(bf16[128,1792]{1,0:T(8,128)(2,1)} %scatter_sum.1) | copy-start | bytes 1376260

commit v5 on v4

--- a/solution.py
+++ b/solution.py
@@ -221,12 +221,9 @@
                 arrived(a, "y", b)
                 copy(a, "core y", b).start()
 
-    lag = 3
-    for i, event in enumerate(events):
+    for event in events:
         plane_event(event)
-        if i >= lag:
-            y_event(events[i - lag])
-    for event in events[len(events) - lag:]:
+    for event in events:
         y_event(event)
 
     for k in keep:
@@ -544,7 +541,7 @@
         ],
         out_specs=[fixed(s) for s in shapes],
         scratch_shapes=[pltpu.VMEM((rows, units), jnp.float32)] * 3,
-        compiler_params=pltpu.CompilerParams(vmem_limit_bytes=40 * 2**20),
+        compiler_params=pltpu.CompilerParams(vmem_limit_bytes=60 * 2**20),
         name="hidden_grads",
     )(tok, cot, w_gate, w_up, w_down, scale)
 

time: 305 us -> 302 us (level)
  local copies, waits for them, and re-layouts: 8.46 us -> 0.78 us
  Pallas kernels: 291 us -> 295 us
    unnamed x13 -> x7, local copies, waits for them, and re-layouts: 8.46 us -> 0.78 us
    pallas_call x1, Pallas kernels: 21.3 us -> 25.4 us  [hidden_grads(): pl.pallas_call(hidden_kernel, grid=(width // tile,), out_shape=[jax.Shape...]
where the time goes in v5:
time: 302 us; the launch traced here: 301 us
  Pallas kernels  295 us (98%)
  other arithmetic  3.98 us (1%)
    pallas_call x1, Pallas kernels, gather_all(): pl.pallas_call(lambda *refs: gather_kernel(members // COLUMNS, held, *ref...  129 us
    pallas_call x1, Pallas kernels, scatter_sum(): pl.pallas_call(lambda *refs: scatter_kernel(depth, *refs), out_shape=jax....  120 us
    pallas_call x1, Pallas kernels, hidden_grads(): pl.pallas_call(hidden_kernel, grid=(width // tile,), out_shape=[jax.Shape...  25.4 us
    pallas_call x1, Pallas kernels, weight_grads(): pl.pallas_call(weight_kernel, grid=(width // tile,), out_shape=[jax.Shape...  21.4 us

profile of v5, /device:TPU:20, one launch (start us, length us, event | category | flops | bytes accessed | tf_op | source)
XLA Modules:
  0.0 300.9 jit_solution(15175748849579682163)
XLA Ops:
  0.6 0.7 convert_element_type.14
  1.3 1.4 select_reduce_fusion
  2.7 128.5 %gather_all.1 = (bf16[128,8,7168]{2,1,0:T(8,128)(2,1)}, bf16[128,8,7168]{2,1,0:T(8,128)(2,1)}, bf16[128,8,128]{2,1,0:T(8,128)(2,1)}) custom-call(bf16[16,8,7168]{2,1,0:T(8,128)(2,1)} %bitcast.23, bf16[16,8,7168]{2,1,0:T(8,128)(2,1)} %bitcast.24, bf16[16,8,128]{2,1,0:T(8,128)(2,1)} %bitcast.26), custom_call_target="tpu_custom_call" | custom-call | tf_op jit(solution)/shard_map/gather_all/pallas_call | solution.py:256
  131.3 1.9 dynamic-slice_convert_fusion.scale
  133.2 25.4 %hidden_grads.1 = (bf16[1024,256]{1,0:T(8,128)(2,1)}, bf16[1024,256]{1,0:T(8,128)(2,1)}, bf16[512,1024]{1,0:T(8,128)(2,1)}, bf16[256,1024]{1,0:T(8,128)(2,1)}) custom-call(bf16[1024,7168]{1,0:T(8,128)(2,1)} %bitcast.14, bf16[1024,7168]{1,0:T(8,128)(2,1)} %bitcast.16, bf16[7168,256]{1,0:T(8,128)(2,1)} %bitcast.18, bf16[7168,256]{1,0:T(8,128)(2,1)} %bitcast.20, ...), custom_call_target="tpu_custom_call" | custom-call | tf_op jit(solution)/shard_map/hidden_grads/pallas_call | solution.py:534
  158.5 0.0 copy-start
  158.6 0.0 copy-start.1
  158.6 120.2 %scatter_sum.1 = bf16[128,1792]{1,0:T(8,128)(2,1)} custom-call(bf16[1024,256]{1,0:T(8,128)(2,1)} %get-tuple-element.17.refs_0_, bf16[1024,256]{1,0:T(8,128)(2,1)} %get-tuple-element.18.refs_1_, bf16[7168,256]{1,0:T(8,128)(2,1)} %bitcast.21, bf16[7168,256]{1,0:T(8,128)(2,1)} %bitcast.19), custom_call_target="tpu_custom_call" | custom-call | tf_op jit(solution)/shard_map/scatter_sum/pallas_call | solution.py:458
  278.7 0.0 copy-done
  278.7 0.0 copy-done.1
  278.7 0.0 copy-start.2
  278.8 21.4 %weight_grads.1 = (bf16[7168,256]{1,0:T(8,128)(2,1)}, bf16[7168,256]{1,0:T(8,128)(2,1)}, bf16[256,7168]{1,0:T(8,128)(2,1)}) custom-call(bf16[1024,7168]{1,0:T(8,128)(2,1)} %bitcast.15, bf16[1024,7168]{1,0:T(8,128)(2,1)} %bitcast.17, bf16[512,1024]{1,0:T(8,128)(2,1)S(1)} %copy-done, bf16[256,1024]{1,0:T(8,128)(2,1)S(1)} %copy-done.1), custom_call_target="tpu_custom_call" | custom-call | tf_op jit(solution)/shard_map/weight_grads/pallas_call | solution.py:564
  300.1 0.0 copy-done.2
  300.1 0.8 copy.14
Async XLA Ops:
  158.5 120.2 %copy-start = (bf16[512,1024]{1,0:T(8,128)(2,1)S(1)}, bf16[512,1024]{1,0:T(8,128)(2,1)}, u32[]{:S(2)}) copy-start(bf16[512,1024]{1,0:T(8,128)(2,1)} %get-tuple-element.19.back_t) | copy-start | bytes 3145732
  158.6 120.2 %copy-start.1 = (bf16[256,1024]{1,0:T(8,128)(2,1)S(1)}, bf16[256,1024]{1,0:T(8,128)(2,1)}, u32[]{:S(2)}) copy-start(bf16[256,1024]{1,0:T(8,128)(2,1)} %get-tuple-element.20.hidden_t) | copy-start | bytes 1572868
  278.7 21.4 %copy-start.2 = (bf16[128,1792]{1,0:T(8,128)(2,1)S(1)}, bf16[128,1792]{1,0:T(8,128)(2,1)}, u32[]{:S(2)}) copy-start(bf16[128,1792]{1,0:T(8,128)(2,1)} %scatter_sum.1) | copy-start | bytes 1376260
